TPU v7x, 512 devices: a whole 4x8x8 slice. The times are simulated.
512 devices in a mesh: lat: 16 (over y_lo, x, core), lon: 32 (over z, y_hi).
Axes of the slice: x: 4, y: 8 (y_hi: 4, y_lo: 2; y = y_hi * 2 + y_lo), z: 8, core: 2. Of those that a mesh axis runs over, the one named last changes fastest.
Arguments:
- features: float32 [4, 96, 384, 192], P(None, 'lat', 'lon'), may hold values from -460 to 460
- cotangent: float32 [4, 96, 384, 192], P(None, 'lat', 'lon'), may hold values from -6 to 6
- norm_gain: float32 [192], replicated, may hold values from 0.1 to 1.9
- norm_shift: float32 [192], replicated, may hold values from -3 to 3
- qkv_weight: float32 [192, 576], replicated, may hold values from -0.4375 to 0.4375
- out_weight: float32 [192, 192], replicated, may hold values from -0.4375 to 0.4375
- bias_table: float32 [16, 2, 6, 23, 144], P('lat'), may hold values from -6 to 305
Outputs:
- grad_features: float32 [4, 96, 384, 192], P(None, 'lat', 'lon')
- grad_weights: float32 [192, 768], P('lat', 'lon')
- grad_bias: float32 [16, 2, 6, 23, 144], P('lat')
- grad_norm: float32 [2, 192], replicated
All inputs are finite; a program needn't handle non-finite values.
Results may differ from a plain program's by a relative error of at most 0.0003.
Values sent between devices are 32-bit elements; how exact they have to be, the bound alone decides.
A program may use at most 128 MiB of HBM per device.

v0:
```python
import math

import jax
import jax.numpy as jnp
from jax import lax
from jax.sharding import PartitionSpec as P

D = 192
HEADS = 6
HEAD = 32
ZP = 4
WZ = 2
WLAT = 6
WLON = 12
PW = 2
WIN = 144
LONREL = 23
PAIRS = 144


EPSILON = 1e-05
HIGH = lax.Precision.HIGHEST


def passed_along(value, axis, steps):
    count = lax.axis_size(axis)
    pairs = [(source, (source + steps) % count) for source in range(count)]
    return lax.ppermute(value, axis, pairs)


def offset_table():
    columns = jnp.arange(WLON, dtype=jnp.int32)
    offset = columns[None, :] - columns[:, None] + (WLON - 1)
    return (offset[:, :, None] == jnp.arange(LONREL, dtype=jnp.int32)[None, None, :]).astype(
        jnp.float32
    )


def level_valid():
    level = jnp.arange(WIN, dtype=jnp.int32) // (WLAT * WLON)
    same_level = level[:, None] == level[None, :]
    window_index = jnp.arange(PW, dtype=jnp.int32)[:, None, None]
    return (window_index > 0) | same_level[None, :, :]


def shards(features, cotangent, norm_gain, norm_shift, qkv_weight, out_weight, bias_table):
    half_cols = WLON // 2
    lat_blocks = features.shape[1] // WLAT
    lon_blocks = features.shape[2] // WLON
    onehot = offset_table()
    score_scale = HEAD ** (-0.5)
    average = jnp.mean(features, -1, keepdims=True)
    centred = features - average
    inverse = lax.rsqrt(jnp.mean(centred * centred, -1, keepdims=True) + EPSILON)
    standard = centred * inverse
    normed = standard * norm_gain + norm_shift
    lifted = jnp.roll(normed, 1, 0)
    upstream = jnp.roll(cotangent, 1, 0)
    borrowed, borrowed_grad = passed_along(
        (lifted[:, :, -half_cols:], upstream[:, :, -half_cols:]), "lon", 1
    )
    joined = jnp.concatenate([borrowed, lifted[:, :, :-half_cols]], axis=2)
    joined_grad = jnp.concatenate([borrowed_grad, upstream[:, :, :-half_cols]], axis=2)

    def to_windows(grid_block):
        shaped = grid_block.reshape(PW, WZ, lat_blocks, WLAT, lon_blocks, WLON, D)
        return shaped.transpose(0, 2, 4, 1, 3, 5, 6).reshape(PW, lat_blocks, lon_blocks, WIN, D)

    def split_heads(tensor):
        return tensor.reshape(PW, lat_blocks, lon_blocks, WIN, HEADS, HEAD)

    hidden_win = to_windows(joined)
    grad_win = to_windows(joined_grad)
    projected = jnp.einsum("plnwd,de->plnwe", hidden_win, qkv_weight, precision=HIGH)
    query_heads = split_heads(projected[..., :D])
    key_heads = split_heads(projected[..., D : 2 * D])
    value_heads = split_heads(projected[..., 2 * D :])
    split_table = bias_table.reshape(lat_blocks, PW, HEADS, LONREL, WZ, WZ, WLAT, WLAT)
    bias_full = jnp.einsum("lchrijab,xyr->clhiaxjby", split_table, onehot, precision=HIGH)
    bias_full = bias_full.reshape(PW, lat_blocks, HEADS, WIN, WIN)
    bias_masked = jnp.where(level_valid()[:, None, None], bias_full, -jnp.inf)
    scores = (
        jnp.einsum("plnahe,plnbhe->plnhab", query_heads, key_heads, precision=HIGH) * score_scale
        + bias_masked[:, :, None]
    )
    row_max = jnp.max(scores, axis=-1, keepdims=True)
    exponent = jnp.exp(scores - row_max)
    attention = exponent * (1.0 / jnp.sum(exponent, axis=-1, keepdims=True))
    mixture = jnp.einsum("plnhab,plnbhe->plnahe", attention, value_heads, precision=HIGH).reshape(
        PW, lat_blocks, lon_blocks, WIN, D
    )
    grad_out_w = jnp.einsum("plnwd,plnwe->de", mixture, grad_win, precision=HIGH)
    grad_mixture = split_heads(jnp.einsum("plnwe,de->plnwd", grad_win, out_weight, precision=HIGH))
    grad_attention = jnp.einsum("plnahe,plnbhe->plnhab", grad_mixture, value_heads, precision=HIGH)
    grad_values = jnp.einsum("plnhab,plnahe->plnbhe", attention, grad_mixture, precision=HIGH)
    grad_scores = attention * (
        grad_attention - jnp.sum(attention * grad_attention, axis=-1, keepdims=True)
    )
    grad_queries = (
        jnp.einsum("plnhab,plnbhe->plnahe", grad_scores, key_heads, precision=HIGH) * score_scale
    )
    grad_keys = (
        jnp.einsum("plnhab,plnahe->plnbhe", grad_scores, query_heads, precision=HIGH) * score_scale
    )
    merged_shape = (PW, lat_blocks, lon_blocks, WIN, D)
    grad_projected = jnp.concatenate(
        [
            grad_queries.reshape(merged_shape),
            grad_keys.reshape(merged_shape),
            grad_values.reshape(merged_shape),
        ],
        axis=-1,
    )
    grad_qkv_w = jnp.einsum("plnwd,plnwe->de", hidden_win, grad_projected, precision=HIGH)
    grad_hidden = jnp.einsum("plnwe,de->plnwd", grad_projected, qkv_weight, precision=HIGH)
    score_sum = jnp.sum(grad_scores, axis=2).reshape(
        PW, lat_blocks, HEADS, WZ, WLAT, WLON, WZ, WLAT, WLON
    )
    bias_local = jnp.einsum("clhiaxjby,xyr->lchrijab", score_sum, onehot, precision=HIGH)
    bias_local = bias_local.reshape(lat_blocks, PW, HEADS, LONREL, PAIRS)
    shaped = grad_hidden.reshape(PW, lat_blocks, lon_blocks, WZ, WLAT, WLON, D)
    back_block = shaped.transpose(0, 3, 1, 4, 2, 5, 6).reshape(
        ZP, lat_blocks * WLAT, lon_blocks * WLON, D
    )
    returned = passed_along(back_block[:, :, :half_cols], "lon", -1)
    grad_lifted = jnp.concatenate([back_block[:, :, half_cols:], returned], axis=2)
    grad_normed = jnp.roll(grad_lifted, -1, 0)
    grad_unit = grad_normed * norm_gain
    grad_features = cotangent + inverse * (
        grad_unit
        - jnp.mean(grad_unit, -1, keepdims=True)
        - standard * jnp.mean(grad_unit * standard, -1, keepdims=True)
    )
    token_count = (
        ZP * features.shape[1] * features.shape[2] * lax.axis_size("lat") * lax.axis_size("lon")
    )
    factor = 1.0 / math.sqrt(token_count)
    norm_local = (
        jnp.stack(
            [jnp.sum(grad_normed * standard, axis=(0, 1, 2)), jnp.sum(grad_normed, axis=(0, 1, 2))]
        )
        * factor
    )
    weights_local = jnp.concatenate([grad_qkv_w, grad_out_w], axis=1) * factor
    grad_bias = lax.psum(bias_local, "lon")
    grad_norm = lax.psum(norm_local, ("lat", "lon"))
    column_part = lax.psum_scatter(weights_local, "lon", scatter_dimension=1, tiled=True)
    grad_weights = lax.psum_scatter(column_part, "lat", scatter_dimension=0, tiled=True)
    return (grad_features, grad_weights, grad_bias, grad_norm)


def solution(mesh):
    placed = (
        P(None, "lat", "lon", None),
        P(None, "lat", "lon", None),
        P(),
        P(),
        P(),
        P(),
        P("lat", None, None, None, None),
    )
    return jax.shard_map(
        shards,
        mesh=mesh,
        in_specs=placed,
        out_specs=(
            P(None, "lat", "lon", None),
            P("lat", "lon"),
            P("lat", None, None, None, None),
            P(),
        ),
        check_vma=False,
    )
```

profile of v0, /device:TPU:6, one launch (start us, length us, event | category | flops | bytes accessed | tf_op | source)
XLA Modules:
  0.0 641.8 jit_solution(16595342032488264519)
XLA Ops:
  9.4 4.5 collective-permute-start.1
  17.6 5.7 collective-permute-start
  24.0 8.9 %convolution_bitcast_fusion = f32[2,1,6,2,6,12,2,6,12]{8,7,4,6,3,2,0,5,1:T(8,128)} fusion(f32[2,6,23,2,2,6,6]{2,0,6,5,4,3,1:T(2,128)S(1)} %bitcast.106, s32[12,12]{1,0:T(8,128)S(1)} %subtract_add_fusion), kind=kOutput, calls=%fused_computation | convolution fusion | flops 68680944 | bytes 1154880 | tf_op jit(solution)/shard_map/lchrijab,xyr->clhiaxjby/dot_general | solution.py:79
  33.0 20.7 %copy.165 = f32[2,1,6,2,6,12,2,6,12]{5,4,3,8,7,6,2,0,1:T(8,128)} copy(f32[2,1,6,2,6,12,2,6,12]{8,7,4,6,3,2,0,5,1:T(8,128)} %convolution_bitcast_fusion) | data formatting | bytes 1990656 | tf_op jit(solution)/shard_map/reshape | solution.py:80
  53.7 10.3 %reshape.280 = f32[2,6,144,144]{2,3,1,0:T(8,128)} reshape(f32[2,1,6,2,6,12,2,6,12]{5,4,3,8,7,6,2,0,1:T(8,128)} %copy.165) | data formatting | bytes 1990656 | tf_op jit(solution)/shard_map/reshape | solution.py:80
  67.2 3.4 fusion.44
  73.6 2.7 fusion.13
  76.3 2.0 multiply_reduce_fusion
  78.8 2.5 convolution_multiply_fusion
  83.1 2.0 fusion.11
  90.8 2.2 copy.168
  95.0 8.6 %reshape.282 = f32[2,6,2,6,12,2,6,12]{4,3,2,7,6,5,1,0:T(8,128)} reshape(f32[2,6,144,144]{2,3,1,0:T(8,128)S(1)} %copy-done.2) | data formatting | bytes 1990656 | tf_op jit(solution)/shard_map/reshape.58
  107.3 8.3 %collective-permute-start.2 = (f32[4,6,6,192]{3,2,1,0:T(8,128)S(1)}, f32[4,6,6,192]{3,2,1,0:T(8,128)S(1)}, u32[]{:S(2)}, u32[]{:S(2)}) collective-permute-start(f32[4,6,6,192]{3,2,1,0:T(8,128)S(1)} %get-tuple-element.35), channel_id=1, source_target_pairs={{0,31},{1,0},{2,1},{3,2},{4,3},{5,4},{6,5},{7,6},{8,7},{9,8},{10,9... | collective-permute-start | bytes 331784 | tf_op jit(solution)/shard_map/ppermute | solution.py:28
  115.6 20.1 %copy.151 = f32[2,6,2,6,12,2,6,12]{7,6,4,5,3,2,1,0:T(8,128)} copy(f32[2,6,2,6,12,2,6,12]{4,3,2,7,6,5,1,0:T(8,128)} %reshape.282) | data formatting | bytes 1990656 | tf_op jit(solution)/shard_map/reshape.58
  135.7 13.0 %convolution_bitcast_fusion.1 = f32[1,2,6,23,2,2,6,6]{3,7,5,6,4,2,1,0:T(8,128)S(1)} fusion(f32[2,6,2,6,12,2,6,12]{7,6,4,5,3,2,1,0:T(8,128)} %copy.151, s32[12,12]{1,0:T(8,128)S(1)} %subtract_add_fusion), kind=kOutput, calls=%fused_computation.7 | convolution fusion | flops 68680944 | bytes 1154880 | tf_op jit(solution)/shard_map/clhiaxjby,xyr->lchrijab/dot_general | solution.py:119
  151.6 166.5 %reduce-scatter.6.cloned.1.call-done = f32[24,192]{1,0:T(8,128)} async-done(((f32[768,192]{1,0:T(8,128)}), f32[24,192]{1,0:T(8,128)}) %reduce-scatter.6.cloned.1.call-update) | async-done | bytes 18448
  318.9 25.3 %fusion = f32[16,24]{1,0:T(8,128)S(1)} fusion(f32[192,24]{1,0:T(8,128)S(1)} %copy.169), kind=kCustom, calls=%all-reduce-scatter | all-reduce-scatter fusion | flops 6145 | bytes 22016
  344.2 4.7 collective-permute-start.5
  348.9 5.6 collective-permute-start.4
  354.5 1.9 collective-permute-start.3
  356.5 1.9 collective-permute-start.6
  359.3 100.7 %psum.15 = f32[2,192]{1,0:T(2,128)} all-reduce(f32[2,192]{1,0:T(2,128)S(1)} %maximum_multiply_fusion.1), channel_id=1, replica_groups=mesh['lat'=16,'lon'=32] {'lat','lon'}, use_global_device_ids=true, to_apply=%region_13.14 | all-reduce | flops 384 | bytes 3072 | tf_op jit(solution)/shard_map/psum | solution.py:146
  460.0 171.7 %all-reduce.4.cloned.1.call-done = f32[1,2,6,23,144]{3,1,4,2,0:T(2,128)} async-done(((f32[1,2,6,23,144]{3,1,4,2,0:T(2,128)}), f32[1,2,6,23,144]{3,1,4,2,0:T(2,128)}) %all-reduce.4.cloned.1.call-update) | async-done | bytes 158992 | tf_op jit(solution)/shard_map/psum | solution.py:145
  631.7 2.2 copy.154
  (102 shorter events, 31.2 us)
Async XLA Ops:
  7.2 57.9 %copy-start = (f32[192,576]{1,0:T(8,128)S(1)}, f32[192,576]{1,0:T(8,128)}, u32[]{:S(2)}) copy-start(f32[192,576]{1,0:T(8,128)} %param.11) | copy-start | bytes 1327108
  7.2 310.9 %reduce-scatter.6.cloned.1.call-start = ((), (), s32[]{:S(2)}) async-start(), calls=%async_computation.2 | async-start | bytes 811008
  8.3 15.0 %copy-start.13 = (f32[1,2,6,23,144]{4,1,3,2,0:T(2,128)S(1)}, f32[1,2,6,23,144]{4,1,3,2,0:T(2,128)}, u32[]{:S(2)}) copy-start(f32[1,2,6,23,144]{4,1,3,2,0:T(2,128)} %param.13) | copy-start | bytes 476932
  9.4 54.6 %collective-permute-start.1 = (f32[4,6,6,192]{3,0,2,1:T(4,128)S(1)}, f32[4,6,6,192]{3,0,2,1:T(4,128)S(1)}, u32[]{:S(2)}, u32[]{:S(2)}) collective-permute-start(f32[4,6,6,192]{3,0,2,1:T(4,128)S(1)} %fusion.30), channel_id=1, source_target_pairs={{0,1},{1,2},{2,3},{3,4},{4,5},{5,6},{6,7},{7,8},{8,9},{9,10},{10,1... | collective-permute-start | bytes 331784 | tf_op jit(solution)/shard_map/ppermute | solution.py:28
  17.6 47.4 %collective-permute-start = (f32[4,6,6,192]{3,2,1,0:T(8,128)S(1)}, f32[4,6,6,192]{3,2,1,0:T(8,128)S(1)}, u32[]{:S(2)}, u32[]{:S(2)}) collective-permute-start(f32[4,6,6,192]{3,2,1,0:T(8,128)S(1)} %fusion.29), channel_id=1, source_target_pairs={{0,1},{1,2},{2,3},{3,4},{4,5},{5,6},{6,7},{7,8},{8,9},{9,10},{10,1... | collective-permute-start | bytes 331784 | tf_op jit(solution)/shard_map/ppermute | solution.py:28
  53.7 10.3 %copy-start.8 = (f32[4,6,12,192]{3,0,2,1:T(4,128)S(1)}, f32[4,6,12,192]{3,0,2,1:T(4,128)}, u32[]{:S(2)}) copy-start(f32[4,6,12,192]{3,0,2,1:T(4,128)} %param.8) | copy-start | bytes 663556
  64.2 1.8 copy-start.7
  65.1 1.9 copy-start.10
  78.8 4.3 copy-start.1
  83.1 3.2 copy-start.4
  83.1 4.7 copy-start.5
  85.2 2.9 copy-start.12
  85.2 3.4 copy-start.11
  89.8 5.2 copy-start.2
  93.0 538.6 %all-reduce.4.cloned.1.call-start = ((), (), s32[]{:S(2)}) async-start(), calls=%async_computation.1 | async-start | bytes 1769472 | tf_op jit(solution)/shard_map/psum | solution.py:145
  103.6 1.0 copy-start.6
  107.3 43.1 %collective-permute-start.2 = (f32[4,6,6,192]{3,2,1,0:T(8,128)S(1)}, f32[4,6,6,192]{3,2,1,0:T(8,128)S(1)}, u32[]{:S(2)}, u32[]{:S(2)}) collective-permute-start(f32[4,6,6,192]{3,2,1,0:T(8,128)S(1)} %get-tuple-element.35), channel_id=1, source_target_pairs={{0,31},{1,0},{2,1},{3,2},{4,3},{5,4},{6,5},{7,6},{8,7},{9,8},{10,9... | collective-permute-start | bytes 331784 | tf_op jit(solution)/shard_map/ppermute | solution.py:28
  148.7 1.8 copy-start.3
  148.7 1.8 copy-start.14
  150.4 1.0 copy-start.9
  344.2 289.7 %collective-permute-start.5 = (f32[16,24]{1,0:T(8,128)S(1)}, f32[16,24]{1,0:T(8,128)S(1)}, u32[]{:S(2)}, u32[]{:S(2)}) collective-permute-start(f32[16,24]{1,0:T(8,128)S(1)} %fusion), channel_id=1, source_target_pairs={{0,96},{32,128},{64,160},{96,192},{128,224},{160,256},{192,288},{2... | collective-permute-start | bytes 4616
  348.9 285.0 %collective-permute-start.4 = (f32[16,24]{1,0:T(8,128)S(1)}, f32[16,24]{1,0:T(8,128)S(1)}, u32[]{:S(2)}, u32[]{:S(2)}) collective-permute-start(f32[16,24]{1,0:T(8,128)S(1)} %fusion), channel_id=1, source_target_pairs={{0,64},{32,96},{64,128},{96,160},{128,192},{160,224},{192,256},{22... | collective-permute-start | bytes 4616
  354.5 279.4 %collective-permute-start.3 = (f32[16,24]{1,0:T(8,128)S(1)}, f32[16,24]{1,0:T(8,128)S(1)}, u32[]{:S(2)}, u32[]{:S(2)}) collective-permute-start(f32[16,24]{1,0:T(8,128)S(1)} %fusion), channel_id=1, source_target_pairs={{0,32},{32,64},{64,96},{96,128},{128,160},{160,192},{192,224},{224... | collective-permute-start | bytes 4616
  356.5 277.4 %collective-permute-start.6 = (f32[12,24]{1,0:T(8,128)S(1)}, f32[12,24]{1,0:T(8,128)S(1)}, u32[]{:S(2)}, u32[]{:S(2)}) collective-permute-start(f32[12,24]{1,0:T(8,128)S(1)} %slice.77), channel_id=1, source_target_pairs={{0,128},{32,160},{64,192},{96,224},{128,256},{160,288},{192,320},{... | collective-permute-start | bytes 3464
Sparse Core Ops, SparseCore 0:
  93.2 224.8 reduce-scatter.5
  321.0 310.6 all-reduce.3
where the time goes:
time: 645 us; the launch traced here: 642 us
  waiting for transfers between devices  338 us (52%)
  blocking collectives  126 us (20%)
  local copies, waits for them, and re-layouts  80.6 us (12%)
  matrix products  41.6 us (6%)
  starting transfers between devices  32.7 us (5%)
  between operations  15.3 us (2%)
  other arithmetic  7.51 us (1%)
    psum x1, waiting for transfers between devices, shards(): grad_bias = lax.psum(bias_local, 'lon')  172 us
    unnamed x7, waiting for transfers between devices  166 us
    psum x1, blocking collectives, shards(): grad_norm = lax.psum(norm_local, ('lat', 'lon'))  101 us
    reshape x2, local copies, waits for them, and re-layouts, shards(): bias_full = bias_full.reshape(PW, lat_blocks, HEADS, WIN, WIN)  30.9 us
    another operation x4, local copies, waits for them, and re-layouts  30.6 us
    unnamed x1, blocking collectives  25.3 us
    ppermute x3, starting transfers between devices, passed_along(): return lax.ppermute(value, axis, pairs)  18.5 us
    unnamed x5, starting transfers between devices  14.2 us
  transfers between devices with their start and end apart: 9, of which 2 were waited for; matrix products, arithmetic and copies ran while one was open for 19% of the time, Pallas kernels for 0%

commit v1 on v0

v1 whole, which is shorter than its diff:
```python
import functools

import jax
import jax.numpy as jnp
import numpy as np
from jax import lax
from jax.experimental import pallas as pl
from jax.experimental.pallas import tpu as pltpu
from jax.sharding import PartitionSpec as P

D = 192
HEADS = 6
HEAD = 32
WLAT = 6
WLON = 12
HALF = WLON // 2
PW = 2
LONREL = 23
PAIRS = 144
EPSILON = 1e-05

GROUP = 16
ROWS = WLON * GROUP
HROWS = HALF * GROUP
STACK = HEADS * ROWS
BLOCK = HEADS * GROUP
STRIP = 24 * GROUP
POS = 12
TABW = 896
NEG = -1e30
F32 = jnp.float32
HIGH = lax.Precision.HIGH
MESH = pl.DeviceIdType.MESH
LAT = 16
NZ = 8
NY = 4
VLIM = 60 * 1024 * 1024


def permutation():
    out = np.zeros((POS * 128, TABW), np.float32)
    for n in range(POS):
        j, b = divmod(n, WLAT)
        for h in range(HEADS):
            for i in range(2):
                for a in range(WLAT):
                    p = ((i * 2 + j) * WLAT + a) * WLAT + b
                    col = h * 128 + p if p < 128 else 768 + h * 16 + p - 128
                    out[n * 128 + h * GROUP + i * 8 + a, col] = 1.0
    return out


def mask_strips():
    lane = np.arange(STRIP) % GROUP
    row = np.arange(BLOCK) % GROUP
    j, b, i = lane // 8, lane % 8, row // 8
    padded = np.broadcast_to((b >= WLAT)[None, :], (BLOCK, STRIP))
    other = i[:, None] != j[None, :]
    return np.where(np.stack([padded | other, padded]), NEG, 0.0).astype(np.float32)


def nn(a, b, precision=HIGH):
    return lax.dot_general(a, b, (((1,), (0,)), ((), ())), precision=precision, preferred_element_type=F32)


def nt(a, b, precision=HIGH):
    return lax.dot_general(a, b, (((1,), (1,)), ((), ())), precision=precision, preferred_element_type=F32)


def tn(a, b, precision=HIGH):
    return lax.dot_general(a, b, (((0,), (0,)), ((), ())), precision=precision, preferred_element_type=F32)


def split(x, terms):
    parts = []
    for _ in range(terms):
        part = x.astype(jnp.bfloat16)
        parts.append(part)
        x = x - part.astype(F32)
    return parts


def pack_piece(feat_ref, cot_ref, slabs, first, store):
    for x in range(HALF):
        for i, z in enumerate(slabs):
            f = feat_ref[pl.ds(z * WLAT, WLAT), first + x, :]
            c = cot_ref[pl.ds(z * WLAT, WLAT), first + x, :]
            value = jnp.concatenate(
                [f[:, :128], c[:, :128], f[:, 128:], c[:, 128:]], axis=1
            )
            value = jnp.concatenate([value, jnp.zeros((2, 2 * D), F32)], axis=0)
            store(x * GROUP + i * 8, value)


def halo_kernel(feat_ref, cot_ref, win_ref, to_right, to_left, send_sem, recv_sem):
    lon = lax.axis_index("lon")
    count = NZ * NY
    right, left = lax.rem(lon + 1, count), lax.rem(lon + count - 1, count)
    barrier = pltpu.get_barrier_semaphore()
    for neighbour in (left, right):
        pl.semaphore_signal(barrier, inc=1, device_id={"lon": neighbour}, device_id_type=MESH)

    def into(ref):
        def store(row, value):
            ref[pl.ds(row, 8), :] = value

        return store

    pack_piece(feat_ref, cot_ref, (3, 0), HALF, into(to_right))
    pack_piece(feat_ref, cot_ref, (1, 2), 0, into(to_left))
    pl.semaphore_wait(barrier, 2)
    copies = [
        pltpu.make_async_remote_copy(
            src_ref=to_right,
            dst_ref=win_ref.at[0, pl.ds(0, HROWS)],
            send_sem=send_sem.at[0],
            recv_sem=recv_sem.at[0],
            device_id={"lon": right},
            device_id_type=MESH,
        ),
        pltpu.make_async_remote_copy(
            src_ref=to_left,
            dst_ref=win_ref.at[1, pl.ds(HROWS, HROWS)],
            send_sem=send_sem.at[1],
            recv_sem=recv_sem.at[1],
            device_id={"lon": left},
            device_id_type=MESH,
        ),
    ]
    for copy in copies:
        copy.start()

    def own(c, base):
        def store(row, value):
            win_ref[c, pl.ds(base + row, 8), :] = value

        return store

    pack_piece(feat_ref, cot_ref, (3, 0), 0, own(0, HROWS))
    pack_piece(feat_ref, cot_ref, (1, 2), HALF, own(1, 0))
    for copy in copies:
        copy.wait()


def halo(features, cotangent):
    vmem = pl.BlockSpec(memory_space=pltpu.VMEM)
    return pl.pallas_call(
        halo_kernel,
        out_shape=jax.ShapeDtypeStruct((PW, ROWS, 2 * D), F32),
        in_specs=[vmem] * 2,
        out_specs=vmem,
        scratch_shapes=[
            pltpu.VMEM((HROWS, 2 * D), F32),
            pltpu.VMEM((HROWS, 2 * D), F32),
            pltpu.SemaphoreType.DMA((2,)),
            pltpu.SemaphoreType.DMA((2,)),
        ],
        compiler_params=pltpu.CompilerParams(collective_id=0, has_side_effects=True, vmem_limit_bytes=VLIM),
        name="halo",
    )(features.reshape(4 * WLAT, WLON, D), cotangent.reshape(4 * WLAT, WLON, D))


def head_lane(h, rows):
    lane = lax.broadcasted_iota(jnp.int32, (rows, D), 1)
    return (lane >= h * HEAD) & (lane < (h + 1) * HEAD)


def compute_kernel(
    win_ref, gain_ref, shift_ref, qkv_ref, out_ref, table_ref, perm_ref, mask_ref,
    grad_ref, wsend_ref, bsend_ref,
    strip, turned, qs, gs, scores, dattn, dstrip, lanes,
):
    zero_row = jnp.zeros((1, 128), F32)
    rem_row = jnp.zeros((1, 16), F32)
    mains, rems = [], []
    for c in range(PW):
        main, rem = [], []
        for h in range(HEADS):
            t = table_ref[c, h]
            main.append(jnp.concatenate([t[:, :128], zero_row], axis=0))
            rem.append(jnp.concatenate([t[:, 128:], rem_row], axis=0))
        rem.append(jnp.zeros((24, 32), F32))
        mains.append(jnp.concatenate(main, axis=1))
        rems.append(jnp.concatenate(rem, axis=1))
    table = jnp.concatenate(
        [jnp.concatenate(mains, axis=0), jnp.concatenate(rems, axis=0)], axis=1
    )
    perm = perm_ref[...]
    spread = sum(nt(part, perm, None) for part in split(table, 3))
    for c in range(PW):
        for n in range(POS):
            row = (n // WLAT) * 8 + n % WLAT
            turned[pl.ds(row, 24, stride=GROUP), :] = spread[c * 24 : c * 24 + 24, n * 128 : n * 128 + 128]
        for n in (6, 7, 14, 15):
            turned[pl.ds(n, 24, stride=GROUP), :] = jnp.zeros((24, 128), F32)
        strip[c] = turned[...].T[:BLOCK, :] + mask_ref[c]

    packed = win_ref[...].reshape(PW * ROWS, 2 * D)
    feat = jnp.concatenate([packed[:, :128], packed[:, 256:320]], axis=1)
    cot = jnp.concatenate([packed[:, 128:256], packed[:, 320:384]], axis=1)
    average = jnp.sum(feat, axis=1, keepdims=True) * (1.0 / D)
    centred = feat - average
    inverse = lax.rsqrt(jnp.sum(centred * centred, axis=1, keepdims=True) * (1.0 / D) + EPSILON)
    unit = centred * inverse
    gain = gain_ref[...]
    hidden = unit * gain + shift_ref[...]
    wq, wk, wv = (qkv_ref[:, e * D : (e + 1) * D] for e in range(3))
    wo = out_ref[...]
    scale = HEAD ** (-0.5)
    query = nn(hidden, wq) * scale
    key = nn(hidden, wk)
    value = nn(hidden, wv)
    grad_mix = nt(cot, wo)

    mixtures, grad_q, grad_k, grad_v = [], [], [], []
    for w in range(PW):
        base = w * ROWS
        q_w, k_w, v_w, g_w = (t[base : base + ROWS] for t in (query, key, value, grad_mix))
        for h in range(HEADS):
            keep = head_lane(h, GROUP)
            for x in range(WLON):
                at = pl.ds(x * BLOCK + h * GROUP, GROUP)
                qs[at, :] = jnp.where(keep, q_w[x * GROUP : (x + 1) * GROUP], 0.0)
                gs[at, :] = jnp.where(keep, g_w[x * GROUP : (x + 1) * GROUP], 0.0)
        scores[...] = nt(qs[...], k_w)
        dattn[...] = nt(gs[...], v_w)
        band = strip[w]
        dband = jnp.zeros((BLOCK, STRIP), F32)
        for x in range(WLON):
            at = pl.ds(x * BLOCK, BLOCK)
            move = (WLON - 1 - x) * GROUP
            bias = band if move == 0 else pltpu.roll(band, STRIP - move, 1)
            s = scores[at, :] + bias[:, :ROWS]
            e = jnp.exp(s - jnp.max(s, axis=1, keepdims=True))
            a = e * (1.0 / jnp.sum(e, axis=1, keepdims=True))
            da = dattn[at, :]
            ds = a * (da - jnp.sum(a * da, axis=1, keepdims=True))
            scores[at, :] = a
            dattn[at, :] = ds
            wide = jnp.concatenate([ds, jnp.zeros((BLOCK, STRIP - ROWS), F32)], axis=1)
            dband = dband + (wide if move == 0 else pltpu.roll(wide, move, 1))
        dstrip[w] = dband
        att = scores[...]
        ds = dattn[...]
        grad_k.append(tn(ds, qs[...]))
        grad_v.append(tn(att, gs[...]))
        for source, other, sink in ((att, v_w, mixtures), (ds, k_w, grad_q)):
            qs[...] = nn(source, other)
            pieces = []
            for x in range(WLON):
                total = jnp.zeros((GROUP, D), F32)
                for h in range(HEADS):
                    total = jnp.where(
                        head_lane(h, GROUP), qs[pl.ds(x * BLOCK + h * GROUP, GROUP), :], total
                    )
                pieces.append(total)
            sink.append(jnp.concatenate(pieces, axis=0))

    mixture = jnp.concatenate(mixtures, axis=0)
    dq = jnp.concatenate(grad_q, axis=0) * scale
    dk = jnp.concatenate(grad_k, axis=0)
    dv = jnp.concatenate(grad_v, axis=0)

    gq, gk, gv = tn(hidden, dq), tn(hidden, dk), tn(hidden, dv)
    go = tn(mixture, cot)
    columns = [
        gq[:, :128], gk[:, :128], gv[:, :128], go[:, :128],
        jnp.concatenate([gq[:, 128:], gk[:, 128:]], axis=1),
        jnp.concatenate([gv[:, 128:], go[:, 128:]], axis=1),
    ]
    for l in range(LAT):
        for g in range(6):
            wsend_ref[l, pl.ds(g * 12, 12), :] = columns[g][l * 12 : (l + 1) * 12]

    gh = nt(dq, wq) + nt(dk, wk) + nt(dv, wv)
    ggain = jnp.sum(gh * unit, axis=0, keepdims=True)
    gshift = jnp.sum(gh, axis=0, keepdims=True)
    norm = jnp.concatenate(
        [
            ggain[:, :128], gshift[:, :128],
            jnp.concatenate([ggain[:, 128:], gshift[:, 128:]], axis=1),
            jnp.zeros((5, 128), F32),
        ],
        axis=0,
    )
    for l in range(LAT):
        wsend_ref[l, pl.ds(72, 8), :] = norm
    gu = gh * gain
    mean_gu = jnp.sum(gu, axis=1, keepdims=True) * (1.0 / D)
    mean_uu = jnp.sum(gu * unit, axis=1, keepdims=True) * (1.0 / D)
    grad_ref[...] = (cot + inverse * (gu - mean_gu - unit * mean_uu)).reshape(PW, ROWS, D)

    for c in range(PW):
        turned[:, :BLOCK] = dstrip[c].T
        for n in range(POS):
            row = (n // WLAT) * 8 + n % WLAT
            lanes[pl.ds(c * 24, 24), n * 128 : n * 128 + 128] = turned[pl.ds(row, 24, stride=GROUP), :]
    sums = sum(nn(part, perm, None) for part in split(lanes[...], 2))
    for t in range(7):
        bsend_ref[t] = sums[:, t * 128 : (t + 1) * 128]
    bsend_ref[7] = jnp.zeros((48, 128), F32)


def compute(win, gain, shift, qkv, out, table, perm, mask):
    vmem = pl.BlockSpec(memory_space=pltpu.VMEM)
    return pl.pallas_call(
        compute_kernel,
        out_shape=(
            jax.ShapeDtypeStruct((PW, ROWS, D), F32),
            jax.ShapeDtypeStruct((LAT, 80, 128), F32),
            jax.ShapeDtypeStruct((NZ, 48, 128), F32),
        ),
        in_specs=[vmem] * 8,
        out_specs=(vmem,) * 3,
        scratch_shapes=[
            pltpu.VMEM((PW, BLOCK, STRIP), F32),
            pltpu.VMEM((STRIP, 128), F32),
            pltpu.VMEM((STACK, D), F32),
            pltpu.VMEM((STACK, D), F32),
            pltpu.VMEM((STACK, ROWS), F32),
            pltpu.VMEM((STACK, ROWS), F32),
            pltpu.VMEM((PW, BLOCK, STRIP), F32),
            pltpu.VMEM((48, POS * 128), F32),
        ],
        compiler_params=pltpu.CompilerParams(vmem_limit_bytes=VLIM),
        name="window_math",
    )(win, gain, shift, qkv, out, table, perm, mask)


def reduce_kernel(
    grad_ref, wsend_ref, bsend_ref,
    feat_ref, weight_ref, bias_ref, norm_ref,
    piece, wrecv, brecv, ypart, yrecv, gathered, zsend, zrecv, ysend, last,
    send_w, recv_w, send_b, recv_b, send_y, recv_y, send_g, recv_g,
    send_z, recv_z, send_l, recv_l, send_p, recv_p,
):
    lat, lon = lax.axis_index("lat"), lax.axis_index("lon")
    count = NZ * NY
    z, y = lon // NY, lax.rem(lon, NY)
    right, left = lax.rem(lon + 1, count), lax.rem(lon + count - 1, count)

    def at_lat(i):
        return {"lat": lax.rem(lat + i, LAT)}

    def at_z(i):
        return {"lon": lax.rem(z + i, NZ) * NY + y}

    def at_y(i):
        return {"lon": z * NY + lax.rem(y + i, NY)}

    barrier = pltpu.get_barrier_semaphore()

    def greet(where):
        def body(i, carry):
            pl.semaphore_signal(barrier, inc=1, device_id=where(i), device_id_type=MESH)
            return carry

        return body

    lax.fori_loop(1, LAT, greet(at_lat), 0)
    lax.fori_loop(1, NZ, greet(at_z), 0)
    lax.fori_loop(1, NY, greet(at_y), 0)
    for neighbour in (left, right):
        pl.semaphore_signal(barrier, inc=1, device_id={"lon": neighbour}, device_id_type=MESH)
    pl.semaphore_wait(barrier, LAT - 1 + NZ - 1 + NY - 1 + 2)

    def remote(src, dst, send, recv, device):
        return pltpu.make_async_remote_copy(
            src_ref=src, dst_ref=dst, send_sem=send, recv_sem=recv, device_id=device, device_id_type=MESH
        )

    def exchange(n, mine, where, src, dst, send, recv):
        def start(i, carry):
            other = lax.rem(mine + i, n)
            remote(src(other), dst.at[mine], send.at[i], recv.at[mine], where(i)).start()
            return carry

        lax.fori_loop(1, n, start, 0)

    def finish(n, mine, where, src, dst, send, recv):
        def done(i, carry):
            other = lax.rem(mine + i, n)
            copy = remote(src(other), dst.at[other], send.at[i], recv.at[other], where(i))
            copy.wait_send()
            copy.wait_recv()
            return carry

        lax.fori_loop(1, n, done, 0)

    def total(ref, n):
        return functools.reduce(lambda a, b: a + b, [ref[s] for s in range(n)])

    step_b = (NZ, z, at_z, lambda o: bsend_ref.at[o], brecv, send_b, recv_b)
    step_w = (LAT, lat, at_lat, lambda o: wsend_ref.at[o], wrecv, send_w, recv_w)
    step_y = (NY, y, at_y, lambda o: ypart, yrecv, send_y, recv_y)
    step_g = (NZ, z, at_z, lambda o: gathered.at[z], gathered, send_g, recv_g)
    step_z = (NZ, z, at_z, lambda o: zsend.at[o], zrecv, send_z, recv_z)
    step_l = (NY, y, at_y, lambda o: ysend, last, send_l, recv_l)

    exchange(*step_b)
    exchange(*step_w)
    backs = [
        remote(grad_ref.at[0, pl.ds(0, HROWS)], piece.at[0], send_p.at[0], recv_p.at[0], {"lon": left}),
        remote(grad_ref.at[1, pl.ds(HROWS, HROWS)], piece.at[1], send_p.at[1], recv_p.at[1], {"lon": right}),
    ]
    for copy in backs:
        copy.start()
    brecv[z] = bsend_ref[z]
    wrecv[lat] = wsend_ref[lat]

    finish(*step_b)
    ypart[...] = total(brecv, NZ)
    yrecv[y] = ypart[...]
    exchange(*step_y)

    finish(*step_w)
    block = total(wrecv, LAT)
    norm = block[72:75]
    lane = lax.broadcasted_iota(jnp.int32, (12, 128), 1)
    for t in range(NZ):
        main = block[(t // 2) * 12 : (t // 2) * 12 + 12]
        if t % 2:
            extra = block[48 + (t // 4) * 12 : 60 + (t // 4) * 12]
            tail = pltpu.roll(extra, 32 if (t // 2) % 2 == 0 else 96, 1)
            main = jnp.where(lane < 32, pltpu.roll(main, 32, 1), tail)
        zsend[t, 0:12, :] = main
        zsend[t, 12:15, :] = norm
        zsend[t, 15:16, :] = jnp.zeros((1, 128), F32)
    zrecv[z] = zsend[z]
    exchange(*step_z)

    finish(*step_y)
    gathered[z] = total(yrecv, NY)
    exchange(*step_g)

    finish(*step_z)
    ysend[...] = total(zrecv, NZ)
    last[y] = ysend[...]
    exchange(*step_l)

    for copy in backs:
        copy.wait()
    for x in range(HALF):
        for c, slabs in ((0, (3, 0)), (1, (1, 2))):
            for i, slab in enumerate(slabs):
                row = x * GROUP + i * 8
                own = grad_ref[c, pl.ds((HROWS if c == 0 else 0) + row, 8), :]
                far = piece[c, pl.ds(row, 8), :]
                west, east = (own, far) if c == 0 else (far, own)
                feat_ref[pl.ds(slab * WLAT, WLAT), x, :] = west[:WLAT]
                feat_ref[pl.ds(slab * WLAT, WLAT), HALF + x, :] = east[:WLAT]

    factor = 1.0 / 384.0
    finish(*step_g)
    for h in range(HEADS):
        main = gathered[h]
        rem = gathered[6]
        rem = rem if h == 0 else pltpu.roll(rem, 128 - 16 * h, 1)
        for c in range(PW):
            bias_ref[c, h, :, 0:128] = main[c * 24 : c * 24 + LONREL]
            bias_ref[c, h, :, 128:144] = rem[c * 24 : c * 24 + LONREL, :16]

    finish(*step_l)
    both = total(last, NY) * factor
    rows = both[0:12]
    mine = rows[:, 0:24]
    for t in range(1, NY):
        mine = jnp.where(y == t, pltpu.roll(rows, 128 - 24 * t, 1)[:, 0:24], mine)
    weight_ref[...] = mine
    norm_ref[0:1, 0:128] = both[12:13]
    norm_ref[1:2, 0:128] = both[13:14]
    norm_ref[0:1, 128:192] = both[14:15, 0:64]
    norm_ref[1:2, 128:192] = both[14:15, 64:128]


def reduce(grad, wsend, bsend):
    vmem = pl.BlockSpec(memory_space=pltpu.VMEM)
    dma = pltpu.SemaphoreType.DMA
    sems = []
    for n in (LAT, NZ, NY, NZ, NZ, NY, 2):
        sems += [dma((n,)), dma((n,))]
    return pl.pallas_call(
        reduce_kernel,
        out_shape=(
            jax.ShapeDtypeStruct((4 * WLAT, WLON, D), F32),
            jax.ShapeDtypeStruct((12, 24), F32),
            jax.ShapeDtypeStruct((PW, HEADS, LONREL, PAIRS), F32),
            jax.ShapeDtypeStruct((2, D), F32),
        ),
        in_specs=[vmem] * 3,
        out_specs=(vmem,) * 4,
        scratch_shapes=[
            pltpu.VMEM((2, HROWS, D), F32),
            pltpu.VMEM((LAT, 80, 128), F32),
            pltpu.VMEM((NZ, 48, 128), F32),
            pltpu.VMEM((48, 128), F32),
            pltpu.VMEM((NY, 48, 128), F32),
            pltpu.VMEM((NZ, 48, 128), F32),
            pltpu.VMEM((NZ, 16, 128), F32),
            pltpu.VMEM((NZ, 16, 128), F32),
            pltpu.VMEM((16, 128), F32),
            pltpu.VMEM((NY, 16, 128), F32),
        ] + sems,
        compiler_params=pltpu.CompilerParams(collective_id=1, has_side_effects=True, vmem_limit_bytes=VLIM),
        name="reductions",
    )(grad, wsend, bsend)


def shards(features, cotangent, norm_gain, norm_shift, qkv_weight, out_weight, bias_table):
    win = halo(features, cotangent)
    grad, wsend, bsend = compute(
        win,
        norm_gain.reshape(1, D),
        norm_shift.reshape(1, D),
        qkv_weight,
        out_weight,
        bias_table.reshape(PW, HEADS, LONREL, PAIRS),
        jnp.asarray(permutation(), jnp.bfloat16),
        jnp.asarray(mask_strips()),
    )
    grad_features, grad_weights, grad_bias, grad_norm = reduce(grad, wsend, bsend)
    return (
        grad_features.reshape(features.shape),
        grad_weights,
        grad_bias.reshape(bias_table.shape),
        grad_norm,
    )


def solution(mesh):
    placed = (
        P(None, "lat", "lon", None),
        P(None, "lat", "lon", None),
        P(),
        P(),
        P(),
        P(),
        P("lat", None, None, None, None),
    )
    return jax.shard_map(
        shards,
        mesh=mesh,
        in_specs=placed,
        out_specs=(
            P(None, "lat", "lon", None),
            P("lat", "lon"),
            P("lat", None, None, None, None),
            P(),
        ),
        check_vma=False,
    )
```

time: 645 us -> 82.2 us (0.13)
  waiting for transfers between devices: 338 us -> 0 us
  blocking collectives: 126 us -> 0 us
  Pallas kernels: 0 us -> 69.3 us
  local copies, waits for them, and re-layouts: 80.6 us -> 11.5 us
  matrix products: 41.6 us -> 0 us
  starting transfers between devices: 32.7 us -> 0 us
  between operations: 15.3 us -> 0.65 us
  other arithmetic: 7.51 us -> 0 us
    psum x1 -> x0, waiting for transfers between devices: 172 us -> none  [shards(): grad_bias = lax.psum(bias_local, 'lon')]
    unnamed x7 -> x0, waiting for transfers between devices: 166 us -> none
    psum x1 -> x0, blocking collectives: 101 us -> none  [shards(): grad_norm = lax.psum(norm_local, ('lat', 'lon'))]
    pallas_call x0 -> x3, Pallas kernels: none -> 69.3 us  [the longest x1 29.4 us: reduce(): pl.pallas_call(reduce_kernel, out_shape=(jax.ShapeDtypeStruct((4 * WLAT,...]
    dot_general x13 -> x0, matrix products: 41.6 us -> none  [the longest x1 13 us: shards(): jnp.einsum('clhiaxjby,xyr->lchrijab', score_sum, onehot, precision=HIGH)]
    reshape x6 -> x0, local copies, waits for them, and re-layouts: 32.7 us -> none  [the longest x2 30.9 us: shards(): bias_full = bias_full.reshape(PW, lat_blocks, HEADS, WIN, WIN)]
    another operation x4 -> x0, local copies, waits for them, and re-layouts: 30.6 us -> none
    unnamed x1 -> x0, blocking collectives: 25.3 us -> none
  transfers between devices with their start and end apart: 9 -> 0, of which waited for: 2 -> 0; matrix products, arithmetic and copies ran while one was open for 19% -> 0% of each run, Pallas kernels for 0% -> 0%
where the time goes in v1:
time: 82.2 us; the launch traced here: 81.5 us
  Pallas kernels  69.3 us (84%)
  local copies, waits for them, and re-layouts  11.5 us (14%)
    pallas_call x1, Pallas kernels, reduce(): pl.pallas_call(reduce_kernel, out_shape=(jax.ShapeDtypeStruct((4 * WLAT,...  29.4 us
    pallas_call x1, Pallas kernels, halo(): pl.pallas_call(halo_kernel, out_shape=jax.ShapeDtypeStruct((PW, ROWS, 2 *...  23.8 us
    pallas_call x1, Pallas kernels, compute(): pl.pallas_call(compute_kernel, out_shape=(jax.ShapeDtypeStruct((PW, ROWS,...  16.1 us
    unnamed x7, local copies, waits for them, and re-layouts  11.5 us

profile of v1, /device:TPU:6, one launch (start us, length us, event | category | flops | bytes accessed | tf_op | source)
XLA Modules:
  0.0 81.5 jit_solution(14617057128622209574)
XLA Ops:
  0.6 1.7 %copy.19 = f32[1,2,6,23,144]{4,3,2,1,0:T(8,128)} copy(f32[1,2,6,23,144]{4,1,3,2,0:T(2,128)} %param.15) | data formatting | bytes 317952 | tf_op args[6]
  2.3 1.8 %copy.13 = f32[4,6,12,192]{3,2,1,0:T(8,128)} copy(f32[4,6,12,192]{3,0,2,1:T(4,128)} %param.9) | data formatting | bytes 442368 | tf_op args[0]
  4.1 1.8 %copy.14 = f32[4,6,12,192]{3,2,1,0:T(8,128)} copy(f32[4,6,12,192]{3,0,2,1:T(4,128)} %param.10) | data formatting | bytes 442368 | tf_op args[1]
  5.9 23.8 %halo.1.win_ref = f32[2,192,384]{2,1,0:T(8,128)} custom-call(f32[24,12,192]{2,1,0:T(8,128)} %bitcast.9, f32[24,12,192]{2,1,0:T(8,128)} %bitcast.10), custom_call_target="tpu_custom_call" | custom-call | tf_op jit(solution)/shard_map/halo/pallas_call | solution.py:147
  29.7 16.1 %window_math.1 = (f32[2,192,192]{2,1,0:T(8,128)}, f32[16,80,128]{2,1,0:T(8,128)}, f32[8,48,128]{2,1,0:T(8,128)}) custom-call(f32[2,192,384]{2,1,0:T(8,128)} %halo.1.win_ref, f32[1,192]{1,0:T(1,128)} %bitcast.14, f32[1,192]{1,0:T(1,128)} %bitcast.15, f32[192,576]{1,0:T(8,128)} %qkv_ref.1, f32[192,192]{1,0:T(8,128)} %out_ref.1, f32[2,6,23,144]{3,2,1,0:T(8,128)} %bitcast.11, ...), custom_call_target="tpu_custom_call" | custom-call | tf_op jit(solution)/shard_map/window_math/pallas_call | solution.py:306
  45.8 29.4 %reductions.1 = (f32[24,12,192]{2,1,0:T(8,128)}, f32[12,24]{1,0:T(8,128)}, f32[2,6,23,144]{3,2,1,0:T(8,128)}, f32[2,192]{1,0:T(2,128)}) custom-call(f32[2,192,192]{2,1,0:T(8,128)} %get-tuple-element.11.grad_ref, f32[16,80,128]{2,1,0:T(8,128)} %get-tuple-element.12.wsend_ref, f32[8,48,128]{2,1,0:T(8,128)} %get-tuple-element.13.bsend_ref), custom_call_target="tpu_custom_call" | custom-call | tf_op jit(solution)/shard_map/reductions/pallas_call | solution.py:482
  75.2 1.9 %copy.16 = f32[4,6,12,192]{3,0,2,1:T(4,128)} copy(f32[4,6,12,192]{3,2,1,0:T(8,128)} %bitcast.12) | data formatting | bytes 442368
  77.1 1.9 %copy.17 = f32[1,2,6,23,144]{4,1,3,2,0:T(2,128)} copy(f32[1,2,6,23,144]{4,3,2,1,0:T(8,128)} %bitcast.13) | data formatting | bytes 317952
  79.0 1.3 %copy.22 = f32[12,24]{1,0:T(8,128)} copy(f32[12,24]{1,0:T(8,128)} %get-tuple-element.27) | data formatting | bytes 2304
  80.3 1.2 %copy.23 = f32[2,192]{1,0:T(2,128)} copy(f32[2,192]{1,0:T(2,128)} %get-tuple-element.29) | data formatting | bytes 3072

commit v2 on v1

v2 whole, which is shorter than its diff:
```python
import functools

import jax
import jax.numpy as jnp
import numpy as np
from jax import lax
from jax.experimental import pallas as pl
from jax.experimental.pallas import tpu as pltpu
from jax.sharding import PartitionSpec as P

D = 192
HEADS = 6
HEAD = 32
WLAT = 6
WLON = 12
HALF = WLON // 2
PW = 2
LONREL = 23
PAIRS = 144
EPSILON = 1e-05

GROUP = 16
ROWS = WLON * GROUP
HROWS = HALF * GROUP
STACK = HEADS * ROWS
BLOCK = HEADS * GROUP
STRIP = 24 * GROUP
POS = 12
TABW = 896
NEG = -1e30
F32 = jnp.float32
HIGH = lax.Precision.HIGH
MESH = pl.DeviceIdType.MESH
LAT = 16
NK = 8
NZ = 8
NY = 4
VLIM = 32 * 1024 * 1024


def permutation():
    out = np.zeros((POS * 128, TABW), np.float32)
    for n in range(POS):
        j, b = divmod(n, WLAT)
        for h in range(HEADS):
            for i in range(2):
                for a in range(WLAT):
                    p = ((i * 2 + j) * WLAT + a) * WLAT + b
                    col = h * 128 + p if p < 128 else 768 + h * 16 + p - 128
                    out[n * 128 + h * GROUP + i * 8 + a, col] = 1.0
    return out


def mask_strips():
    lane = np.arange(STRIP) % GROUP
    row = np.arange(BLOCK) % GROUP
    j, b, i = lane // 8, lane % 8, row // 8
    padded = np.broadcast_to((b >= WLAT)[None, :], (BLOCK, STRIP))
    other = i[:, None] != j[None, :]
    return np.where(np.stack([padded | other, padded]), NEG, 0.0).astype(np.float32)


def nn(a, b, precision=HIGH):
    return lax.dot_general(a, b, (((1,), (0,)), ((), ())), precision=precision, preferred_element_type=F32)


def nt(a, b, precision=HIGH):
    return lax.dot_general(a, b, (((1,), (1,)), ((), ())), precision=precision, preferred_element_type=F32)


def tn(a, b, precision=HIGH):
    return lax.dot_general(a, b, (((0,), (0,)), ((), ())), precision=precision, preferred_element_type=F32)


def split(x, terms):
    parts = []
    for _ in range(terms):
        part = x.astype(jnp.bfloat16)
        parts.append(part)
        x = x - part.astype(F32)
    return parts


def pack_piece(feat_ref, cot_ref, slabs, first, store):
    for x in range(HALF):
        for i, z in enumerate(slabs):
            f = feat_ref[:, first + x, z, :]
            c = cot_ref[:, first + x, z, :]
            value = jnp.concatenate(
                [f[:, :128], c[:, :128], f[:, 128:], c[:, 128:]], axis=1
            )
            value = jnp.concatenate([value, jnp.zeros((2, 2 * D), F32)], axis=0)
            store(x * GROUP + i * 8, value)


def head_lane(h, rows):
    lane = lax.broadcasted_iota(jnp.int32, (rows, D), 1)
    return (lane >= h * HEAD) & (lane < (h + 1) * HEAD)


def bias_strips(table_ref, perm_ref, mask_ref, turned, strip):
    zero_row = jnp.zeros((1, 128), F32)
    rem_row = jnp.zeros((1, 16), F32)
    mains, rems = [], []
    for c in range(PW):
        main, rem = [], []
        for h in range(HEADS):
            t = table_ref[h, :, c, :]
            main.append(jnp.concatenate([t[:, :128], zero_row], axis=0))
            rem.append(jnp.concatenate([t[:, 128:], rem_row], axis=0))
        rem.append(jnp.zeros((24, 32), F32))
        mains.append(jnp.concatenate(main, axis=1))
        rems.append(jnp.concatenate(rem, axis=1))
    table = jnp.concatenate(
        [jnp.concatenate(mains, axis=0), jnp.concatenate(rems, axis=0)], axis=1
    )
    perm = perm_ref[...]
    spread = sum(nt(part, perm, None) for part in split(table, 3))
    for c in range(PW):
        for n in range(POS):
            row = (n // WLAT) * 8 + n % WLAT
            turned[pl.ds(row, 24, stride=GROUP), :] = spread[c * 24 : c * 24 + 24, n * 128 : n * 128 + 128]
        for n in (6, 7, 14, 15):
            turned[pl.ds(n, 24, stride=GROUP), :] = jnp.zeros((24, 128), F32)
        strip[c] = turned[...].T[:BLOCK, :] + mask_ref[c]


def main_kernel(
    comm,
    feat_ref, cot_ref, gain_ref, shift_ref, qkv_ref, out_ref, table_ref, perm_ref, mask_ref,
    grad_ref, piece, gathered, last,
    win, to_right, to_left, hid, unit, cot, inv, que, key, val, gmx,
    strip, turned, qs, gs, scores, dattn, dstrip, lanes,
    wsend, nsend, bsend, crecv, nrecv, csum, hrecv, brecv, ypart, yrecv, zsend, zrecv, ysend,
    send_p, recv_p, send_c, recv_c, send_h, recv_h, send_b, recv_b, send_y, recv_y, send_g, recv_g,
    send_z, recv_z, send_l, recv_l,
):
    if comm:
        lat, lon = lax.axis_index("lat"), lax.axis_index("lon")
    else:
        lat, lon = jnp.int32(0), jnp.int32(0)
    count = NZ * NY
    z, y = lon // NY, lax.rem(lon, NY)
    k, core = lat // 2, lax.rem(lat, 2)
    right, left = {"lon": lax.rem(lon + 1, count)}, {"lon": lax.rem(lon + count - 1, count)}
    partner = {"lat": k * 2 + 1 - core}

    def at_k(i):
        return {"lat": lax.rem(k + i, NK) * 2 + core}

    def at_z(i):
        return {"lon": lax.rem(z + i, NZ) * NY + y}

    def at_y(i):
        return {"lon": z * NY + lax.rem(y + i, NY)}

    def remote(src, dst, send, recv, device):
        return pltpu.make_async_remote_copy(
            src_ref=src, dst_ref=dst, send_sem=send, recv_sem=recv, device_id=device, device_id_type=MESH
        )

    def start_all(copies):
        for copy in copies if comm else ():
            copy.start()

    def wait_all(copies):
        for copy in copies if comm else ():
            copy.wait()

    def exchange(n, mine, where, src, dst, send, recv):
        def start(i, carry):
            other = lax.rem(mine + i, n)
            remote(src(other), dst.at[mine], send.at[i], recv.at[mine], where(i)).start()
            return carry

        if comm:
            lax.fori_loop(1, n, start, 0)

    def finish(n, mine, where, src, dst, send, recv):
        def done(i, carry):
            other = lax.rem(mine + i, n)
            copy = remote(src(other), dst.at[other], send.at[i], recv.at[other], where(i))
            copy.wait_send()
            copy.wait_recv()
            return carry

        if comm:
            lax.fori_loop(1, n, done, 0)

    def total(ref, n):
        return functools.reduce(lambda a, b: a + b, [ref[s] for s in range(n)])

    if comm:
        barrier = pltpu.get_barrier_semaphore()

        def greet(where):
            def step(i, carry):
                pl.semaphore_signal(barrier, inc=1, device_id=where(i), device_id_type=MESH)
                return carry

            return step

        for device in (left, right, partner):
            pl.semaphore_signal(barrier, inc=1, device_id=device, device_id_type=MESH)
        lax.fori_loop(1, NY, greet(at_y), 0)
        lax.fori_loop(1, NZ, greet(at_z), 0)
        lax.fori_loop(1, NK, greet(at_k), 0)

    def into(ref, base):
        def store(row, value):
            ref[pl.ds(base + row, 8), :] = value

        return store

    pack_piece(feat_ref, cot_ref, (3, 0), HALF, into(to_right, 0))
    pack_piece(feat_ref, cot_ref, (1, 2), 0, into(to_left, 0))
    if comm:
        pl.semaphore_wait(barrier, 3 + NY - 1 + NZ - 1 + NK - 1)
    halo = [
        remote(to_right, win.at[pl.ds(0, HROWS)], send_p.at[0], recv_p.at[0], right),
        remote(to_left, win.at[pl.ds(3 * HROWS, HROWS)], send_p.at[1], recv_p.at[1], left),
    ]
    start_all(halo)
    if not comm:
        win[pl.ds(0, HROWS), :] = to_right[...]
        win[pl.ds(3 * HROWS, HROWS), :] = to_left[...]
    pack_piece(feat_ref, cot_ref, (3, 0), 0, into(win, HROWS))
    pack_piece(feat_ref, cot_ref, (1, 2), HALF, into(win, 2 * HROWS))

    gain = gain_ref[...]
    shift = shift_ref[...]
    wq, wk, wv = (qkv_ref[:, e * D : (e + 1) * D] for e in range(3))
    wo = out_ref[...]
    scale = HEAD ** (-0.5)

    def project(first, rows):
        at = pl.ds(first, rows)
        packed = win[at, :]
        f = jnp.concatenate([packed[:, :128], packed[:, 256:320]], axis=1)
        c = jnp.concatenate([packed[:, 128:256], packed[:, 320:384]], axis=1)
        centred = f - jnp.sum(f, axis=1, keepdims=True) * (1.0 / D)
        inverse = lax.rsqrt(jnp.sum(centred * centred, axis=1, keepdims=True) * (1.0 / D) + EPSILON)
        standard = centred * inverse
        hidden = standard * gain + shift
        cot[at, :] = c
        unit[at, :] = standard
        inv[at, :] = inverse
        hid[at, :] = hidden
        que[at, :] = nn(hidden, wq) * scale
        key[at, :] = nn(hidden, wk)
        val[at, :] = nn(hidden, wv)
        gmx[at, :] = nt(c, wo)

    project(HROWS, 2 * HROWS)
    bias_strips(table_ref, perm_ref, mask_ref, turned, strip)
    wait_all(halo)
    project(0, HROWS)
    project(3 * HROWS, HROWS)

    mixtures, grad_q, grad_k, grad_v = [], [], [], []
    for w in range(PW):
        own = pl.ds(w * ROWS, ROWS)
        q_w, k_w, v_w, g_w = que[own, :], key[own, :], val[own, :], gmx[own, :]
        for h in range(HEADS):
            keep = head_lane(h, GROUP)
            for x in range(WLON):
                at = pl.ds(x * BLOCK + h * GROUP, GROUP)
                qs[at, :] = jnp.where(keep, q_w[x * GROUP : (x + 1) * GROUP], 0.0)
                gs[at, :] = jnp.where(keep, g_w[x * GROUP : (x + 1) * GROUP], 0.0)
        scores[...] = nt(qs[...], k_w)
        dattn[...] = nt(gs[...], v_w)
        band = strip[w]
        dband = jnp.zeros((BLOCK, STRIP), F32)
        for x in range(WLON):
            at = pl.ds(x * BLOCK, BLOCK)
            move = (WLON - 1 - x) * GROUP
            bias = band if move == 0 else pltpu.roll(band, STRIP - move, 1)
            s = scores[at, :] + bias[:, :ROWS]
            e = jnp.exp(s - jnp.max(s, axis=1, keepdims=True))
            a = e * (1.0 / jnp.sum(e, axis=1, keepdims=True))
            da = dattn[at, :]
            ds = a * (da - jnp.sum(a * da, axis=1, keepdims=True))
            scores[at, :] = a
            dattn[at, :] = ds
            wide = jnp.concatenate([ds, jnp.zeros((BLOCK, STRIP - ROWS), F32)], axis=1)
            dband = dband + (wide if move == 0 else pltpu.roll(wide, move, 1))
        turned[:, :BLOCK] = dband.T
        for n in range(POS):
            row = (n // WLAT) * 8 + n % WLAT
            lanes[pl.ds(w * 24, 24), n * 128 : n * 128 + 128] = turned[pl.ds(row, 24, stride=GROUP), :]
        if w == PW - 1:
            perm = perm_ref[...]
            sums = sum(nn(part, perm, None) for part in split(lanes[...], 2))
            for t in range(7):
                bsend[t] = sums[:, t * 128 : (t + 1) * 128]
            bsend[7] = jnp.zeros((48, 128), F32)
            step_b = (NZ, z, at_z, lambda o: bsend.at[o], brecv, send_b, recv_b)
            exchange(*step_b)
        att = scores[...]
        ds = dattn[...]
        grad_k.append(tn(ds, qs[...]))
        grad_v.append(tn(att, gs[...]))
        for source, other, sink in ((att, v_w, mixtures), (ds, k_w, grad_q)):
            qs[...] = nn(source, other)
            pieces = []
            for x in range(WLON):
                both = jnp.zeros((GROUP, D), F32)
                for h in range(HEADS):
                    both = jnp.where(
                        head_lane(h, GROUP), qs[pl.ds(x * BLOCK + h * GROUP, GROUP), :], both
                    )
                pieces.append(both)
            sink.append(jnp.concatenate(pieces, axis=0))

    mixture = jnp.concatenate(mixtures, axis=0)
    dq = jnp.concatenate(grad_q, axis=0) * scale
    dk = jnp.concatenate(grad_k, axis=0)
    dv = jnp.concatenate(grad_v, axis=0)

    hidden = hid[...]
    gq, gk, gv = tn(hidden, dq), tn(hidden, dk), tn(hidden, dv)
    go = tn(mixture, cot[...])
    columns = [
        gq[:, :128], gk[:, :128], gv[:, :128], go[:, :128],
        jnp.concatenate([gq[:, 128:], gk[:, 128:]], axis=1),
        jnp.concatenate([gv[:, 128:], go[:, 128:]], axis=1),
    ]
    for l in range(LAT):
        for g in range(6):
            wsend[l % 2, l // 2, pl.ds(g * 12, 12), :] = columns[g][l * 12 : (l + 1) * 12]
    swap = [remote(wsend.at[1 - core], crecv, send_c.at[0], recv_c.at[0], partner)]
    start_all(swap)

    gh = nt(dq, wq) + nt(dk, wk) + nt(dv, wv)
    standard = unit[...]
    ggain = jnp.sum(gh * standard, axis=0, keepdims=True)
    gshift = jnp.sum(gh, axis=0, keepdims=True)
    nsend[...] = jnp.concatenate(
        [
            ggain[:, :128], gshift[:, :128],
            jnp.concatenate([ggain[:, 128:], gshift[:, 128:]], axis=1),
            jnp.zeros((5, 128), F32),
        ],
        axis=0,
    )
    swap.append(remote(nsend, nrecv, send_c.at[1], recv_c.at[1], partner))
    start_all(swap[1:])
    gu = gh * gain
    mean_gu = jnp.sum(gu, axis=1, keepdims=True) * (1.0 / D)
    mean_uu = jnp.sum(gu * standard, axis=1, keepdims=True) * (1.0 / D)
    grad_ref[...] = cot[...] + inv[...] * (gu - mean_gu - standard * mean_uu)
    backs = [
        remote(grad_ref.at[pl.ds(0, HROWS)], piece.at[0], send_p.at[2], recv_p.at[2], left),
        remote(grad_ref.at[pl.ds(3 * HROWS, HROWS)], piece.at[1], send_p.at[3], recv_p.at[3], right),
    ]
    start_all(backs)
    if not comm:
        gathered[...] = bsend[...]
        hrecv[:, 0:72, :] = wsend[0]
        csum[:, 0:72, :] = wsend[1]
        hrecv[0, 72:80, :] = nsend[...]
        return

    step_y = (NY, y, at_y, lambda o: ypart, yrecv, send_y, recv_y)
    step_g = (NZ, z, at_z, lambda o: gathered.at[z], gathered, send_g, recv_g)
    step_h = (NK, k, at_k, lambda o: csum.at[o], hrecv, send_h, recv_h)
    step_z = (NZ, z, at_z, lambda o: zsend.at[o], zrecv, send_z, recv_z)
    step_l = (NY, y, at_y, lambda o: ysend, last, send_l, recv_l)

    wait_all(swap)
    both = nsend[...] + nrecv[...]
    for o in range(NK):
        csum[o, 0:72, :] = wsend[core, o] + crecv[o]
        csum[o, 72:80, :] = both
    exchange(*step_h)
    hrecv[k] = csum[k]

    brecv[z] = bsend[z]
    finish(*step_b)
    ypart[...] = total(brecv, NZ)
    exchange(*step_y)
    yrecv[y] = ypart[...]

    finish(*step_h)
    block = total(hrecv, NK)
    norm = block[72:75]
    lane = lax.broadcasted_iota(jnp.int32, (12, 128), 1)
    for t in range(NZ):
        main = block[(t // 2) * 12 : (t // 2) * 12 + 12]
        if t % 2:
            extra = block[48 + (t // 4) * 12 : 60 + (t // 4) * 12]
            tail = pltpu.roll(extra, 32 if (t // 2) % 2 == 0 else 96, 1)
            main = jnp.where(lane < 32, pltpu.roll(main, 32, 1), tail)
        zsend[t, 0:12, :] = main
        zsend[t, 12:15, :] = norm
        zsend[t, 15:16, :] = jnp.zeros((1, 128), F32)
    exchange(*step_z)
    zrecv[z] = zsend[z]

    finish(*step_y)
    gathered[z] = total(yrecv, NY)
    exchange(*step_g)

    finish(*step_z)
    ysend[...] = total(zrecv, NZ)
    exchange(*step_l)
    last[y] = ysend[...]

    wait_all(backs)
    finish(*step_g)
    finish(*step_l)


def main_call(comm, operands):
    vmem = pl.BlockSpec(memory_space=pltpu.VMEM)
    dma = pltpu.SemaphoreType.DMA
    sems = []
    for n in (4, 2, NK, NZ, NY, NZ, NZ, NY):
        sems += [dma((n,)), dma((n,))]

    def buf(*shape):
        return pltpu.VMEM(shape, F32)

    full = buf(PW * ROWS, D)
    wsend, csum, hrecv = buf(2, NK, 72, 128), buf(NK, 80, 128), buf(NK, 80, 128)
    params = dict(vmem_limit_bytes=VLIM)
    if comm:
        params.update(collective_id=0, has_side_effects=True)
    return pl.pallas_call(
        functools.partial(main_kernel, comm),
        out_shape=(
            jax.ShapeDtypeStruct((PW * ROWS, D), F32),
            jax.ShapeDtypeStruct((PW, HROWS, D), F32),
            jax.ShapeDtypeStruct((NZ, 48, 128), F32),
            jax.ShapeDtypeStruct((NY, 16, 128), F32),
        ),
        in_specs=[vmem] * 9,
        out_specs=(vmem,) * 4,
        scratch_shapes=[
            buf(PW * ROWS, 2 * D), buf(HROWS, 2 * D), buf(HROWS, 2 * D),
            full, full, full, buf(PW * ROWS, 1), full, full, full, full,
            buf(PW, BLOCK, STRIP), buf(STRIP, 128),
            buf(STACK, D), buf(STACK, D), buf(STACK, ROWS), buf(STACK, ROWS),
            buf(PW, BLOCK, STRIP), buf(48, POS * 128),
            wsend, buf(8, 128), buf(NZ, 48, 128), buf(NK, 72, 128), buf(8, 128), csum, hrecv,
            buf(NZ, 48, 128), buf(48, 128), buf(NY, 48, 128),
            buf(NZ, 16, 128), buf(NZ, 16, 128), buf(16, 128),
        ] + sems,
        compiler_params=pltpu.CompilerParams(**params),
        name="window_block",
    )(*operands)


def unpack_kernel(grad_ref, piece, gathered, last, feat_ref, weight_ref, bias_ref, norm_ref):
    y = lax.rem(lax.axis_index("lon"), NY)
    for x in range(HALF):
        for c, slabs in ((0, (3, 0)), (1, (1, 2))):
            for i, slab in enumerate(slabs):
                row = x * GROUP + i * 8
                own = grad_ref[pl.ds((1 + c) * HROWS + row, 8), :]
                far = piece[c, pl.ds(row, 8), :]
                west, east = (own, far) if c == 0 else (far, own)
                feat_ref[:, x, slab, :] = west[:WLAT]
                feat_ref[:, HALF + x, slab, :] = east[:WLAT]
    for h in range(HEADS):
        main = gathered[h]
        rem = gathered[6]
        rem = rem if h == 0 else pltpu.roll(rem, 128 - 16 * h, 1)
        for c in range(PW):
            bias_ref[h, :, c, 0:128] = main[c * 24 : c * 24 + LONREL]
            bias_ref[h, :, c, 128:144] = rem[c * 24 : c * 24 + LONREL, :16]
    both = functools.reduce(lambda a, b: a + b, [last[s] for s in range(NY)]) * (1.0 / 384.0)
    rows = both[0:12]
    mine = rows[:, 0:24]
    for t in range(1, NY):
        mine = jnp.where(y == t, pltpu.roll(rows, 128 - 24 * t, 1)[:, 0:24], mine)
    weight_ref[...] = mine
    norm_ref[0:1, 0:128] = both[12:13]
    norm_ref[1:2, 0:128] = both[13:14]
    norm_ref[0:1, 128:192] = both[14:15, 0:64]
    norm_ref[1:2, 128:192] = both[14:15, 64:128]


def unpack(operands):
    vmem = pl.BlockSpec(memory_space=pltpu.VMEM)
    return pl.pallas_call(
        unpack_kernel,
        out_shape=(
            jax.ShapeDtypeStruct((WLAT, WLON, 4, D), F32),
            jax.ShapeDtypeStruct((12, 24), F32),
            jax.ShapeDtypeStruct((HEADS, LONREL, PW, PAIRS), F32),
            jax.ShapeDtypeStruct((2, D), F32),
        ),
        in_specs=[vmem] * 4,
        out_specs=(vmem,) * 4,
        compiler_params=pltpu.CompilerParams(vmem_limit_bytes=8 * 1024 * 1024),
        name="unpack",
    )(*operands)


def operands_of(features, cotangent, norm_gain, norm_shift, qkv_weight, out_weight, bias_table):
    return (
        features.transpose(1, 2, 0, 3),
        cotangent.transpose(1, 2, 0, 3),
        norm_gain.reshape(1, D),
        norm_shift.reshape(1, D),
        qkv_weight,
        out_weight,
        bias_table.reshape(PW, HEADS, LONREL, PAIRS).transpose(1, 2, 0, 3),
        jnp.asarray(permutation(), jnp.bfloat16),
        jnp.asarray(mask_strips()),
    )


def shards(*args):
    grad_features, grad_weights, grad_bias, grad_norm = unpack(main_call(True, operands_of(*args)))
    return (
        grad_features.transpose(2, 0, 1, 3),
        grad_weights,
        grad_bias.transpose(2, 0, 1, 3).reshape(1, PW, HEADS, LONREL, PAIRS),
        grad_norm,
    )


def solution(mesh):
    placed = (
        P(None, "lat", "lon", None),
        P(None, "lat", "lon", None),
        P(),
        P(),
        P(),
        P(),
        P("lat", None, None, None, None),
    )
    return jax.shard_map(
        shards,
        mesh=mesh,
        in_specs=placed,
        out_specs=(
            P(None, "lat", "lon", None),
            P("lat", "lon"),
            P("lat", None, None, None, None),
            P(),
        ),
        check_vma=False,
    )
```

time: 82.2 us -> 67.7 us (0.82)
  Pallas kernels: 69.3 us -> 57.7 us
  local copies, waits for them, and re-layouts: 11.5 us -> 8.93 us
    pallas_call x3 -> x2, Pallas kernels: 69.3 us -> 57.7 us  [the longest x1 56.7 us: main_call(): pl.pallas_call(functools.partial(main_kernel, comm), out_shape=(jax.Shape...]
    unnamed x7 -> x18, local copies, waits for them, and re-layouts: 11.5 us -> 8.93 us
where the time goes in v2:
time: 67.7 us; the launch traced here: 67.3 us
  Pallas kernels  57.7 us (85%)
  local copies, waits for them, and re-layouts  8.93 us (13%)
    pallas_call x1, Pallas kernels, main_call(): pl.pallas_call(functools.partial(main_kernel, comm), out_shape=(jax.Shape...  56.7 us
    unnamed x18, local copies, waits for them, and re-layouts  8.93 us

profile of v2, /device:TPU:6, one launch (start us, length us, event | category | flops | bytes accessed | tf_op | source)
XLA Modules:
  0.0 67.3 jit_solution(16745632415636406911)
XLA Ops:
  0.6 0.0 copy-start
  0.6 1.8 %copy-done = bf16[1536,896]{1,0:T(8,128)(2,1)S(1)} copy-done((bf16[1536,896]{1,0:T(8,128)(2,1)S(1)}, bf16[1536,896]{1,0:T(8,128)(2,1)}, u32[]{:S(2)}) %copy-start) | copy-done | bytes 2752536
  2.4 0.0 copy-start.1
  2.4 1.0 %copy-done.1 = f32[192,576]{1,0:T(8,128)S(1)} copy-done((f32[192,576]{1,0:T(8,128)S(1)}, f32[192,576]{1,0:T(8,128)}, u32[]{:S(2)}) %copy-start.1) | copy-done | bytes 442392
  3.4 0.0 copy-start.2
  3.4 1.0 %copy-done.2 = f32[4,6,12,192]{3,0,2,1:T(4,128)S(1)} copy-done((f32[4,6,12,192]{3,0,2,1:T(4,128)S(1)}, f32[4,6,12,192]{3,0,2,1:T(4,128)}, u32[]{:S(2)}) %copy-start.2) | copy-done | bytes 221208
  4.4 0.0 copy-start.3
  4.4 1.0 %copy-done.3 = f32[4,6,12,192]{3,0,2,1:T(4,128)S(1)} copy-done((f32[4,6,12,192]{3,0,2,1:T(4,128)S(1)}, f32[4,6,12,192]{3,0,2,1:T(4,128)}, u32[]{:S(2)}) %copy-start.3) | copy-done | bytes 221208
  5.4 0.0 copy-start.4
  5.4 1.0 %copy-done.4 = f32[2,96,384]{2,1,0:T(8,128)S(1)} copy-done((f32[2,96,384]{2,1,0:T(8,128)S(1)}, f32[2,96,384]{2,1,0:T(8,128)}, u32[]{:S(2)}) %copy-start.4) | copy-done | bytes 294936
  6.3 0.0 copy-start.5
  6.3 1.0 %copy-done.5 = f32[1,2,6,23,144]{4,1,3,2,0:T(2,128)S(1)} copy-done((f32[1,2,6,23,144]{4,1,3,2,0:T(2,128)S(1)}, f32[1,2,6,23,144]{4,1,3,2,0:T(2,128)}, u32[]{:S(2)}) %copy-start.5) | copy-done | bytes 159000
  7.3 0.0 copy-start.6
  7.3 0.9 %copy-done.6 = f32[192,192]{1,0:T(8,128)S(1)} copy-done((f32[192,192]{1,0:T(8,128)S(1)}, f32[192,192]{1,0:T(8,128)}, u32[]{:S(2)}) %copy-start.6) | copy-done | bytes 147480
  8.2 0.0 copy-start.7
  8.2 0.7 %copy-done.7 = f32[192]{0:T(256)S(1)} copy-done((f32[192]{0:T(256)S(1)}, f32[192]{0:T(256)}, u32[]{:S(2)}) %copy-start.7) | copy-done | bytes 792
  8.9 0.0 copy-start.8
  8.9 0.7 %copy-done.8 = f32[192]{0:T(256)S(1)} copy-done((f32[192]{0:T(256)S(1)}, f32[192]{0:T(256)}, u32[]{:S(2)}) %copy-start.8) | copy-done | bytes 792
  9.6 56.7 %window_block.1 = (f32[384,192]{1,0:T(8,128)S(1)}, f32[2,96,192]{2,1,0:T(8,128)S(1)}, f32[8,48,128]{2,1,0:T(8,128)S(1)}, f32[4,16,128]{2,1,0:T(8,128)S(1)}) custom-call(f32[6,12,4,192]{3,2,1,0:T(4,128)S(1)} %bitcast.11, f32[6,12,4,192]{3,2,1,0:T(4,128)S(1)} %bitcast.12, f32[1,192]{1,0:T(1,128)S(1)} %bitcast.14, f32[1,192]{1,0:T(1,128)S(1)} %bitcast.15, ...), custom_call_target="tpu_custom_call" | custom-call | tf_op jit(solution)/shard_map/window_block/pallas_call | solution.py:429
  66.3 1.0 %unpack.1 = (f32[6,12,4,192]{3,2,1,0:T(4,128)}, f32[12,24]{1,0:T(8,128)}, f32[6,23,2,144]{3,2,1,0:T(2,128)}, f32[2,192]{1,0:T(2,128)}) custom-call(f32[384,192]{1,0:T(8,128)S(1)} %get-tuple-element.12.grad_ref, f32[2,96,192]{2,1,0:T(8,128)S(1)} %get-tuple-element.13.piece, f32[8,48,128]{2,1,0:T(8,128)S(1)} %get-tuple-element.14.gathered, ...), custom_call_target="tpu_custom_call" | custom-call | tf_op jit(solution)/shard_map/unpack/pallas_call | solution.py:486
Async XLA Ops:
  0.6 1.8 %copy-start = (bf16[1536,896]{1,0:T(8,128)(2,1)S(1)}, bf16[1536,896]{1,0:T(8,128)(2,1)}, u32[]{:S(2)}) copy-start(bf16[1536,896]{1,0:T(8,128)(2,1)} %constant.4.clone.perm_ref) | copy-start | bytes 8257540
  2.4 1.0 %copy-start.1 = (f32[192,576]{1,0:T(8,128)S(1)}, f32[192,576]{1,0:T(8,128)}, u32[]{:S(2)}) copy-start(f32[192,576]{1,0:T(8,128)} %qkv_ref.1) | copy-start | bytes 1327108
  3.4 1.0 %copy-start.2 = (f32[4,6,12,192]{3,0,2,1:T(4,128)S(1)}, f32[4,6,12,192]{3,0,2,1:T(4,128)}, u32[]{:S(2)}) copy-start(f32[4,6,12,192]{3,0,2,1:T(4,128)} %param.9) | copy-start | bytes 663556
  4.4 1.0 %copy-start.3 = (f32[4,6,12,192]{3,0,2,1:T(4,128)S(1)}, f32[4,6,12,192]{3,0,2,1:T(4,128)}, u32[]{:S(2)}) copy-start(f32[4,6,12,192]{3,0,2,1:T(4,128)} %param.10) | copy-start | bytes 663556
  5.4 1.0 %copy-start.4 = (f32[2,96,384]{2,1,0:T(8,128)S(1)}, f32[2,96,384]{2,1,0:T(8,128)}, u32[]{:S(2)}) copy-start(f32[2,96,384]{2,1,0:T(8,128)} %constant.5.clone.mask_ref) | copy-start | bytes 884740
  6.3 1.0 %copy-start.5 = (f32[1,2,6,23,144]{4,1,3,2,0:T(2,128)S(1)}, f32[1,2,6,23,144]{4,1,3,2,0:T(2,128)}, u32[]{:S(2)}) copy-start(f32[1,2,6,23,144]{4,1,3,2,0:T(2,128)} %param.15) | copy-start | bytes 476932
  7.3 0.9 %copy-start.6 = (f32[192,192]{1,0:T(8,128)S(1)}, f32[192,192]{1,0:T(8,128)}, u32[]{:S(2)}) copy-start(f32[192,192]{1,0:T(8,128)} %out_ref.1) | copy-start | bytes 442372
  8.2 0.7 %copy-start.7 = (f32[192]{0:T(256)S(1)}, f32[192]{0:T(256)}, u32[]{:S(2)}) copy-start(f32[192]{0:T(256)} %param.11) | copy-start | bytes 2308
  8.9 0.7 %copy-start.8 = (f32[192]{0:T(256)S(1)}, f32[192]{0:T(256)}, u32[]{:S(2)}) copy-start(f32[192]{0:T(256)} %param.12) | copy-start | bytes 2308

commit v3 on v2

v3 whole, which is shorter than its diff:
```python
import functools

import jax
import jax.numpy as jnp
import numpy as np
from jax import lax
from jax.experimental import pallas as pl
from jax.experimental.pallas import tpu as pltpu
from jax.sharding import PartitionSpec as P

D = 192
HEADS = 6
HEAD = 32
WLAT = 6
WLON = 12
HALF = WLON // 2
PW = 2
LONREL = 23
PAIRS = 144
EPSILON = 1e-05

GROUP = 16
ROWS = WLON * GROUP
HROWS = HALF * GROUP
PSTACK = 2 * ROWS
PIECES = 2 * HALF
BF16 = jnp.bfloat16
BLOCK = HEADS * GROUP
STRIP = 24 * GROUP
POS = 12
TABW = 896
NEG = -1e30
PAIRS_OF_HEADS = 3
LANES = 2 * HEAD
F32 = jnp.float32
HIGH = lax.Precision.HIGH
MESH = pl.DeviceIdType.MESH
LAT = 16
NK = 8
NZ = 8
NY = 4
VLIM = 32 * 1024 * 1024


def permutation():
    out = np.zeros((POS * 128, TABW), np.float32)
    for n in range(POS):
        j, b = divmod(n, WLAT)
        for h in range(HEADS):
            for i in range(2):
                for a in range(WLAT):
                    p = ((i * 2 + j) * WLAT + a) * WLAT + b
                    col = h * 128 + p if p < 128 else 768 + h * 16 + p - 128
                    out[n * 128 + h * GROUP + i * 8 + a, col] = 1.0
    return out


def nn(a, b, precision=HIGH):
    return lax.dot_general(a, b, (((1,), (0,)), ((), ())), precision=precision, preferred_element_type=F32)


def nt(a, b, precision=HIGH):
    return lax.dot_general(a, b, (((1,), (1,)), ((), ())), precision=precision, preferred_element_type=F32)


def tn(a, b, precision=HIGH):
    return lax.dot_general(a, b, (((0,), (0,)), ((), ())), precision=precision, preferred_element_type=F32)


def split(x, terms):
    parts = []
    for _ in range(terms):
        part = x.astype(jnp.bfloat16)
        parts.append(part)
        x = x - part.astype(F32)
    return parts


def strip_mask(c):
    lane = lax.broadcasted_iota(jnp.int32, (BLOCK, STRIP), 1)
    row = lax.broadcasted_iota(jnp.int32, (BLOCK, STRIP), 0)
    shut = (lane & 7) >= WLAT
    if c == 0:
        shut = shut | (((lane >> 3) & 1) != ((row >> 3) & 1))
    return jnp.where(shut, NEG, 0.0)


def bias_strips(table_ref, perm_ref, turned, strip):
    zero_row = jnp.zeros((1, 128), F32)
    rem_row = jnp.zeros((1, 16), F32)
    mains, rems = [], []
    for c in range(PW):
        main, rem = [], []
        for h in range(HEADS):
            t = table_ref[h, :, c, :]
            main.append(jnp.concatenate([t[:, :128], zero_row], axis=0))
            rem.append(jnp.concatenate([t[:, 128:], rem_row], axis=0))
        rem.append(jnp.zeros((24, 32), F32))
        mains.append(jnp.concatenate(main, axis=1))
        rems.append(jnp.concatenate(rem, axis=1))
    table = jnp.concatenate(
        [jnp.concatenate(mains, axis=0), jnp.concatenate(rems, axis=0)], axis=1
    )
    perm = perm_ref[...]
    spread = sum(nt(part, perm, None) for part in split(table, 3))
    for c in range(PW):
        for n in range(POS):
            row = (n // WLAT) * 8 + n % WLAT
            turned[pl.ds(row, 24, stride=GROUP), :] = spread[c * 24 : c * 24 + 24, n * 128 : n * 128 + 128]
        for n in (6, 7, 14, 15):
            turned[pl.ds(n, 24, stride=GROUP), :] = jnp.zeros((24, 128), F32)
        strip[c] = turned[...].T[:BLOCK, :] + strip_mask(c)


def parity_lanes(width):
    lane = lax.broadcasted_iota(jnp.int32, (1, width), 1)
    second = ((lane >> 5) & 1).astype(F32)
    return (1.0 - second).astype(BF16), second.astype(BF16)


def pair_rows(high, low, p):
    lanes = slice(p * LANES, (p + 1) * LANES)
    joined = jnp.concatenate([high[:, lanes], low[:, lanes], high[:, lanes]], axis=1)
    first, second = parity_lanes(3 * LANES)
    cells = joined.reshape(WLON, GROUP, 3 * LANES)
    return jnp.concatenate([cells * first, cells * second], axis=1).reshape(PSTACK, 3 * LANES)


def pair_cols(high, low, p):
    lanes = slice(p * LANES, (p + 1) * LANES)
    return jnp.concatenate([high[:, lanes], high[:, lanes], low[:, lanes]], axis=1)


def pick_heads(value):
    cells = value.reshape(WLON, 2 * GROUP, LANES)
    lane = lax.broadcasted_iota(jnp.int32, (WLON, GROUP, LANES), 2)
    return jnp.where(lane < HEAD, cells[:, :GROUP], cells[:, GROUP:]).reshape(ROWS, LANES)


def main_kernel(
    comm,
    feat_hbm, cot_hbm, gain_hbm, shift_hbm, qkv_hbm, out_hbm, table_hbm, perm_hbm,
    *refs,
):
    if not comm:
        spare, refs = refs[4], refs[:4] + refs[5:]
    (
        grad_ref, piece, gathered, last,
        feat_ref, cot_ref, gain_ref, shift_ref, qkv_ref, out_ref, table_ref, perm_ref, load_sem,
        halo_out, halo_in, win, back_out, unit, cot, inv, hid,
        qh, ql, kh, kl, vh, vl, gh_, gl_,
        strip, turned, qst, gst, scores, dattn, ah, al, dh, dl, lanes,
        wsend, xsend, nsend, bsend, wcore, xcore, ncore, wsum, xsum, wrecv, xrecv,
        brecv, ypart, yrecv, zsend, zrecv, ysend,
        send_p, recv_p, send_c, recv_c, send_h, recv_h, send_x, recv_x, send_b, recv_b,
        send_y, recv_y, send_g, recv_g, send_z, recv_z, send_l, recv_l,
    ) = refs
    loads = [
        pltpu.make_async_copy(src, dst, load_sem.at[i])
        for i, (src, dst) in enumerate(
            (
                (feat_hbm, feat_ref), (cot_hbm, cot_ref), (gain_hbm, gain_ref), (shift_hbm, shift_ref),
                (qkv_hbm, qkv_ref), (out_hbm, out_ref), (table_hbm, table_ref), (perm_hbm, perm_ref),
            )
        )
    ]
    for load in loads:
        load.start()
    if comm:
        lat, lon = lax.axis_index("lat"), lax.axis_index("lon")
    else:
        lat, lon = jnp.int32(0), jnp.int32(0)
    count = NZ * NY
    z, y = lon // NY, lax.rem(lon, NY)
    k, core = lat // 2, lax.rem(lat, 2)
    right, left = {"lon": lax.rem(lon + 1, count)}, {"lon": lax.rem(lon + count - 1, count)}
    partner = {"lat": k * 2 + 1 - core}

    def at_k(i):
        return {"lat": lax.rem(k + i, NK) * 2 + core}

    def at_z(i):
        return {"lon": lax.rem(z + i, NZ) * NY + y}

    def at_y(i):
        return {"lon": z * NY + lax.rem(y + i, NY)}

    def remote(src, dst, send, recv, device):
        return pltpu.make_async_remote_copy(
            src_ref=src, dst_ref=dst, send_sem=send, recv_sem=recv, device_id=device, device_id_type=MESH
        )

    def start_all(copies):
        for copy in copies if comm else ():
            copy.start()

    def wait_all(copies):
        for copy in copies if comm else ():
            copy.wait()

    def exchange(n, mine, where, src, dst, send, recv):
        def start(i, carry):
            other = lax.rem(mine + i, n)
            remote(src(other), dst.at[mine], send.at[i], recv.at[mine], where(i)).start()
            return carry

        if comm:
            lax.fori_loop(1, n, start, 0)

    def finish(n, mine, where, src, dst, send, recv):
        def done(i, carry):
            other = lax.rem(mine + i, n)
            copy = remote(src(other), dst.at[other], send.at[i], recv.at[other], where(i))
            copy.wait_send()
            copy.wait_recv()
            return carry

        if comm:
            lax.fori_loop(1, n, done, 0)

    def total(ref, n):
        return functools.reduce(lambda a, b: a + b, [ref[s] for s in range(n)])

    if comm:
        barrier = pltpu.get_barrier_semaphore()

        def greet(where):
            def step(i, carry):
                pl.semaphore_signal(barrier, inc=1, device_id=where(i), device_id_type=MESH)
                return carry

            return step

        lax.fori_loop(1, NY, greet(at_y), 0)
        lax.fori_loop(1, NZ, greet(at_z), 0)
        lax.fori_loop(1, NK, greet(at_k), 0)
        for device in (left, right, partner):
            pl.semaphore_signal(barrier, inc=1, device_id=device, device_id_type=MESH)

    def tiles(slabs, first):
        for x in range(HALF):
            for i, slab in enumerate(slabs):
                f = feat_ref[:, first + x, slab, :]
                c = cot_ref[:, first + x, slab, :]
                mixed = jnp.concatenate([f[:, 128:], c[:, 128:]], axis=1)
                yield x * 2 + i, (f[:, :128], mixed, c[:, :128])

    loads[0].wait()
    loads[1].wait()
    for d, (slabs, first) in enumerate((((3, 0), HALF), ((1, 2), 0))):
        for g, parts in tiles(slabs, first):
            for t in range(3):
                halo_out[d, t * PIECES + g] = parts[t]
    if comm:
        pl.semaphore_wait(barrier, 3 + NY - 1 + NZ - 1 + NK - 1)
    cuts = (pl.ds(0, 2 * PIECES), pl.ds(2 * PIECES, PIECES))
    halo = [
        [
            remote(halo_out.at[d, cut], halo_in.at[d, cut], send_p.at[2 * e + d], recv_p.at[2 * e + d], (right, left)[d])
            for d in range(2)
        ]
        for e, cut in enumerate(cuts)
    ]
    start_all(halo[0])
    start_all(halo[1])
    gap = jnp.zeros((2, 128), F32)
    for base, slabs, first in ((HROWS, (3, 0), 0), (2 * HROWS, (1, 2), HALF)):
        for g, parts in tiles(slabs, first):
            for t in range(3):
                win[t, pl.ds(base + g * 8, 8), :] = jnp.concatenate([parts[t], gap], axis=0)

    def arrived(which):
        for d, base in ((0, 0), (1, 3 * HROWS)):
            for t in which:
                for g in range(PIECES):
                    source = halo_in if comm else halo_out
                    win[t, pl.ds(base + g * 8, 8), :] = jnp.concatenate(
                        [source[d, t * PIECES + g], gap], axis=0
                    )

    for load in loads[2:6]:
        load.wait()
    gain = gain_ref[...]
    shift = shift_ref[...]
    wq, wk, wv = (qkv_ref[:, e * D : (e + 1) * D] for e in range(3))
    wo = out_ref[...]
    scale = HEAD ** (-0.5)

    def keep(at, value, high, low):
        high[at, :], low[at, :] = split(value, 2)

    def project_features(first, rows):
        at = pl.ds(first, rows)
        f = jnp.concatenate([win[0, at, :], win[1, at, :][:, :64]], axis=1)
        centred = f - jnp.sum(f, axis=1, keepdims=True) * (1.0 / D)
        inverse = lax.rsqrt(jnp.sum(centred * centred, axis=1, keepdims=True) * (1.0 / D) + EPSILON)
        standard = centred * inverse
        hidden = standard * gain + shift
        unit[at, :] = standard
        inv[at, :] = inverse
        hid[at, :] = hidden
        keep(at, nn(hidden, wq) * scale, qh, ql)
        keep(at, nn(hidden, wk), kh, kl)
        keep(at, nn(hidden, wv), vh, vl)

    def project_cotangent(first, rows):
        at = pl.ds(first, rows)
        c = jnp.concatenate([win[2, at, :], win[1, at, :][:, 64:]], axis=1)
        cot[at, :] = c
        keep(at, nt(c, wo), gh_, gl_)

    project_features(HROWS, 2 * HROWS)
    project_cotangent(HROWS, 2 * HROWS)
    loads[6].wait()
    loads[7].wait()
    bias_strips(table_ref, perm_ref, turned, strip)

    wait_all(halo[0])
    arrived((0, 1))
    project_features(0, HROWS)
    project_features(3 * HROWS, HROWS)
    windows = [pl.ds(w * ROWS, ROWS) for w in range(PW)]
    for w, own in enumerate(windows):
        for p in range(PAIRS_OF_HEADS):
            rows = pair_rows(qh[own, :], ql[own, :], p)
            qst[w, p] = rows
            part = nt(rows, pair_cols(kh[own, :], kl[own, :], p), None)
            scores[w, :, p * 32 : p * 32 + 32, :] = part.reshape(WLON, 32, ROWS)

    wait_all(halo[1])
    arrived((2,))
    project_cotangent(0, HROWS)
    project_cotangent(3 * HROWS, HROWS)
    for w, own in enumerate(windows):
        for p in range(PAIRS_OF_HEADS):
            rows = pair_rows(gh_[own, :], gl_[own, :], p)
            gst[w, p] = rows
            part = nt(rows, pair_cols(vh[own, :], vl[own, :], p), None)
            dattn[w, :, p * 32 : p * 32 + 32, :] = part.reshape(WLON, 32, ROWS)

    for w in range(PW):
        band = strip[w]
        dband = jnp.zeros((BLOCK, STRIP), F32)
        for x in range(WLON):
            move = (WLON - 1 - x) * GROUP
            bias = band if move == 0 else pltpu.roll(band, STRIP - move, 1)
            s = scores[w, x] + bias[:, :ROWS]
            e = jnp.exp(s - jnp.max(s, axis=1, keepdims=True))
            a = e * (1.0 / jnp.sum(e, axis=1, keepdims=True))
            da = dattn[w, x]
            ds = a * (da - jnp.sum(a * da, axis=1, keepdims=True))
            ah[w, x], al[w, x] = split(a, 2)
            dh[w, x], dl[w, x] = split(ds, 2)
            wide = jnp.concatenate([ds, jnp.zeros((BLOCK, STRIP - ROWS), F32)], axis=1)
            dband = dband + (wide if move == 0 else pltpu.roll(wide, move, 1))
        turned[:, :BLOCK] = dband.T
        for n in range(POS):
            row = (n // WLAT) * 8 + n % WLAT
            lanes[pl.ds(w * 24, 24), n * 128 : n * 128 + 128] = turned[pl.ds(row, 24, stride=GROUP), :]

    def pair_of(ref, w, p):
        return ref[w, :, p * 32 : p * 32 + 32, :].reshape(PSTACK, ROWS)

    def applied(high, low, other_high, other_low):
        result = []
        for w, own in enumerate(windows):
            cols = []
            for p in range(PAIRS_OF_HEADS):
                at = slice(p * LANES, (p + 1) * LANES)
                oh = other_high[own, :][:, at]
                both = nn(pair_of(high, w, p), jnp.concatenate([oh, other_low[own, :][:, at]], axis=1), None)
                rest = nn(pair_of(low, w, p), oh, None)
                cols.append(pick_heads(both[:, :LANES] + both[:, LANES:] + rest))
            result.append(jnp.concatenate(cols, axis=1))
        return jnp.concatenate(result, axis=0)

    def gathered_keys(high, low, stack):
        result = []
        for w in range(PW):
            cols = []
            for p in range(PAIRS_OF_HEADS):
                rows = stack[w, p]
                both = tn(pair_of(high, w, p), rows[:, : 2 * LANES], None)
                rest = tn(pair_of(low, w, p), rows[:, :LANES], None)
                cols.append(both[:, :LANES] + both[:, LANES:] + rest)
            result.append(jnp.concatenate(cols, axis=1))
        return jnp.concatenate(result, axis=0)

    def cut(ref, one, two):
        columns = [
            one[:, :128], two[:, :128],
            jnp.concatenate([one[:, 128:], two[:, 128:]], axis=1),
        ]
        for l in range(LAT):
            for g in range(3):
                ref[l % 2, l // 2, pl.ds(g * 12, 12), :] = columns[g][l * 12 : (l + 1) * 12]

    mixture = applied(ah, al, vh, vl)
    dv = gathered_keys(ah, al, gst)
    hidden = hid[...]
    cut(wsend, tn(hidden, dv), tn(mixture, cot[...]))
    swap = [
        remote(wsend.at[1 - core], wcore, send_c.at[0], recv_c.at[0], partner),
        remote(xsend.at[1 - core], xcore, send_c.at[1], recv_c.at[1], partner),
        remote(nsend, ncore, send_c.at[2], recv_c.at[2], partner),
    ]
    start_all(swap[:1])

    perm = perm_ref[...]
    sums = sum(nn(part, perm, None) for part in split(lanes[...], 2))
    for t in range(7):
        bsend[t] = sums[:, t * 128 : (t + 1) * 128]
    bsend[7] = jnp.zeros((48, 128), F32)
    step_b = (NZ, z, at_z, lambda o: bsend.at[o], brecv, send_b, recv_b)
    exchange(*step_b)

    dq = applied(dh, dl, kh, kl) * scale
    step_h = (NK, k, at_k, lambda o: wsum.at[o], wrecv, send_h, recv_h)
    step_x = (NK, k, at_k, lambda o: xsum.at[o], xrecv, send_x, recv_x)
    wait_all(swap[:1])
    if comm:
        for o in range(NK):
            wsum[o] = wsend[core, o] + wcore[o]
        exchange(*step_h)
        wrecv[k] = wsum[k]

    dk = gathered_keys(dh, dl, qst)
    cut(xsend, tn(hidden, dq), tn(hidden, dk))
    start_all(swap[1:2])

    gh = nt(dq, wq) + nt(dk, wk) + nt(dv, wv)
    standard = unit[...]
    ggain = jnp.sum(gh * standard, axis=0, keepdims=True)
    gshift = jnp.sum(gh, axis=0, keepdims=True)
    nsend[...] = jnp.concatenate(
        [
            ggain[:, :128], gshift[:, :128],
            jnp.concatenate([ggain[:, 128:], gshift[:, 128:]], axis=1),
            jnp.zeros((1, 128), F32),
        ],
        axis=0,
    )
    start_all(swap[2:])
    wait_all(swap[1:])
    if comm:
        for o in range(NK):
            xsum[o, 0:36, :] = xsend[core, o] + xcore[o]
            xsum[o, 36:40, :] = nsend[...] + ncore[...]
        exchange(*step_x)
        xrecv[k] = xsum[k]

    gu = gh * gain
    mean_gu = jnp.sum(gu, axis=1, keepdims=True) * (1.0 / D)
    mean_uu = jnp.sum(gu * standard, axis=1, keepdims=True) * (1.0 / D)
    grad_ref[...] = cot[...] + inv[...] * (gu - mean_gu - standard * mean_uu)
    for d, base in ((0, 0), (1, 3 * HROWS)):
        for g in range(PIECES):
            back_out[d, g] = grad_ref[pl.ds(base + g * 8, WLAT), :]
    backs = [
        remote(back_out.at[d], piece.at[d], send_p.at[4 + d], recv_p.at[4 + d], (left, right)[d])
        for d in range(2)
    ]
    start_all(backs)
    if not comm:
        gathered[...] = bsend[...]
        spare[0] = wsend[...]
        spare[1] = xsend[...]
        last[0, 0:4, :] = nsend[...]
        return

    step_y = (NY, y, at_y, lambda o: ypart, yrecv, send_y, recv_y)
    step_g = (NZ, z, at_z, lambda o: gathered.at[z], gathered, send_g, recv_g)
    step_z = (NZ, z, at_z, lambda o: zsend.at[o], zrecv, send_z, recv_z)
    step_l = (NY, y, at_y, lambda o: ysend, last, send_l, recv_l)

    brecv[z] = bsend[z]
    finish(*step_b)
    ypart[...] = total(brecv, NZ)
    exchange(*step_y)
    yrecv[y] = ypart[...]

    finish(*step_h)
    block_vo = total(wrecv, NK)
    finish(*step_x)
    block_qk = total(xrecv, NK)
    norm = block_qk[36:39]
    lane = lax.broadcasted_iota(jnp.int32, (12, 128), 1)
    for t in range(NZ):
        block = block_qk if t < 4 else block_vo
        e = (t // 2) % 2
        main = block[e * 12 : e * 12 + 12]
        if t % 2:
            tail = pltpu.roll(block[24:36], 96 if e else 32, 1)
            main = jnp.where(lane < 32, pltpu.roll(main, 32, 1), tail)
        zsend[t, 0:12, :] = main
        zsend[t, 12:15, :] = norm
        zsend[t, 15:16, :] = jnp.zeros((1, 128), F32)
    exchange(*step_z)
    zrecv[z] = zsend[z]

    finish(*step_y)
    gathered[z] = total(yrecv, NY)
    exchange(*step_g)

    finish(*step_z)
    ysend[...] = total(zrecv, NZ)
    exchange(*step_l)
    last[y] = ysend[...]

    wait_all(backs)
    finish(*step_g)
    finish(*step_l)


def main_call(comm, operands):
    vmem = pl.BlockSpec(memory_space=pltpu.VMEM)
    hbm = pl.BlockSpec(memory_space=pltpu.HBM)
    dma = pltpu.SemaphoreType.DMA
    sems = []
    for n in (6, 3, NK, NK, NZ, NY, NZ, NZ, NY):
        sems += [dma((n,)), dma((n,))]

    def buf(*shape):
        return pltpu.VMEM(shape, F32)

    def half(*shape):
        return pltpu.VMEM(shape, BF16)

    full = buf(PW * ROWS, D)
    token = half(PW * ROWS, D)
    stack = half(PW, PAIRS_OF_HEADS, PSTACK, 3 * LANES)
    square = (PW, WLON, BLOCK, ROWS)
    outs = (
        jax.ShapeDtypeStruct((PW * ROWS, D), F32),
        jax.ShapeDtypeStruct((PW, PIECES, WLAT, D), F32),
        jax.ShapeDtypeStruct((NZ, 48, 128), F32),
        jax.ShapeDtypeStruct((NY, 16, 128), F32),
    )
    params = dict(vmem_limit_bytes=VLIM)
    if comm:
        params.update(collective_id=0, has_side_effects=True)
    else:
        outs += (jax.ShapeDtypeStruct((2, 2, NK, 36, 128), F32),)
    return pl.pallas_call(
        functools.partial(main_kernel, comm),
        out_shape=outs,
        in_specs=[hbm] * 8,
        out_specs=(vmem,) * len(outs),
        scratch_shapes=[pltpu.VMEM(t.shape, t.dtype) for t in operands] + [
            dma((8,)),
            buf(2, 3 * PIECES, WLAT, 128), buf(2, 3 * PIECES, WLAT, 128), buf(3, PW * ROWS, 128),
            buf(2, PIECES, WLAT, D),
            full, full, buf(PW * ROWS, 1), full,
            token, token, token, token, token, token, token, token,
            buf(PW, BLOCK, STRIP), buf(STRIP, 128), stack, stack, buf(*square), buf(*square),
            half(*square), half(*square), half(*square), half(*square), buf(48, POS * 128),
            buf(2, NK, 36, 128), buf(2, NK, 36, 128), buf(4, 128), buf(NZ, 48, 128),
            buf(NK, 36, 128), buf(NK, 36, 128), buf(4, 128),
            buf(NK, 36, 128), buf(NK, 40, 128), buf(NK, 36, 128), buf(NK, 40, 128),
            buf(NZ, 48, 128), buf(48, 128), buf(NY, 48, 128),
            buf(NZ, 16, 128), buf(NZ, 16, 128), buf(16, 128),
        ] + sems,
        compiler_params=pltpu.CompilerParams(**params),
        name="window_block",
    )(*(pltpu.with_memory_space_constraint(t, pltpu.HBM) for t in operands))


def unpack_kernel(grad_ref, piece, gathered, last, feat_ref, weight_ref, bias_ref, norm_ref):
    y = lax.rem(lax.axis_index("lon"), NY)
    for x in range(HALF):
        for c, slabs in ((0, (3, 0)), (1, (1, 2))):
            for i, slab in enumerate(slabs):
                row = x * GROUP + i * 8
                own = grad_ref[pl.ds((1 + c) * HROWS + row, 8), :]
                own, far = own[:WLAT], piece[c, x * 2 + i]
                west, east = (own, far) if c == 0 else (far, own)
                feat_ref[:, x, slab, :] = west
                feat_ref[:, HALF + x, slab, :] = east
    for h in range(HEADS):
        main = gathered[h]
        rem = gathered[6]
        rem = rem if h == 0 else pltpu.roll(rem, 128 - 16 * h, 1)
        for c in range(PW):
            bias_ref[h, :, c, 0:128] = main[c * 24 : c * 24 + LONREL]
            bias_ref[h, :, c, 128:144] = rem[c * 24 : c * 24 + LONREL, :16]
    both = functools.reduce(lambda a, b: a + b, [last[s] for s in range(NY)]) * (1.0 / 384.0)
    rows = both[0:12]
    mine = rows[:, 0:24]
    for t in range(1, NY):
        mine = jnp.where(y == t, pltpu.roll(rows, 128 - 24 * t, 1)[:, 0:24], mine)
    weight_ref[...] = mine
    norm_ref[0:1, 0:128] = both[12:13]
    norm_ref[1:2, 0:128] = both[13:14]
    norm_ref[0:1, 128:192] = both[14:15, 0:64]
    norm_ref[1:2, 128:192] = both[14:15, 64:128]


def unpack(operands):
    vmem = pl.BlockSpec(memory_space=pltpu.VMEM)
    return pl.pallas_call(
        unpack_kernel,
        out_shape=(
            jax.ShapeDtypeStruct((WLAT, WLON, 4, D), F32),
            jax.ShapeDtypeStruct((12, 24), F32),
            jax.ShapeDtypeStruct((HEADS, LONREL, PW, PAIRS), F32),
            jax.ShapeDtypeStruct((2, D), F32),
        ),
        in_specs=[vmem] * 4,
        out_specs=(vmem,) * 4,
        compiler_params=pltpu.CompilerParams(vmem_limit_bytes=8 * 1024 * 1024),
        name="unpack",
    )(*operands)


def operands_of(features, cotangent, norm_gain, norm_shift, qkv_weight, out_weight, bias_table):
    return (
        features.transpose(1, 2, 0, 3),
        cotangent.transpose(1, 2, 0, 3),
        norm_gain.reshape(1, D),
        norm_shift.reshape(1, D),
        qkv_weight,
        out_weight,
        bias_table.reshape(PW, HEADS, LONREL, PAIRS).transpose(1, 2, 0, 3),
        jnp.asarray(permutation(), jnp.bfloat16),
    )


def shards(*args):
    grad_features, grad_weights, grad_bias, grad_norm = unpack(main_call(True, operands_of(*args)))
    return (
        grad_features.transpose(2, 0, 1, 3),
        grad_weights,
        grad_bias.transpose(2, 0, 1, 3).reshape(1, PW, HEADS, LONREL, PAIRS),
        grad_norm,
    )


def solution(mesh):
    placed = (
        P(None, "lat", "lon", None),
        P(None, "lat", "lon", None),
        P(),
        P(),
        P(),
        P(),
        P("lat", None, None, None, None),
    )
    return jax.shard_map(
        shards,
        mesh=mesh,
        in_specs=placed,
        out_specs=(
            P(None, "lat", "lon", None),
            P("lat", "lon"),
            P("lat", None, None, None, None),
            P(),
        ),
        check_vma=False,
    )
```

time: 67.7 us -> 56.9 us (0.84)
  local copies, waits for them, and re-layouts: 8.93 us -> 0 us
  Pallas kernels: 57.7 us -> 55.4 us
    unnamed x18 -> x0, local copies, waits for them, and re-layouts: 8.93 us -> none
    pallas_call x1, Pallas kernels: 56.7 us -> 54.4 us  [main_call(): pl.pallas_call(functools.partial(main_kernel, comm), out_shape=outs, in_s...]
where the time goes in v3:
time: 56.9 us; the launch traced here: 56 us
  Pallas kernels  55.4 us (97%)
  between operations  0.64 us (1%)
    pallas_call x1, Pallas kernels, main_call(): pl.pallas_call(functools.partial(main_kernel, comm), out_shape=outs, in_s...  54.4 us

profile of v3, /device:TPU:6, one launch (start us, length us, event | category | flops | bytes accessed | tf_op | source)
XLA Modules:
  0.0 56.0 jit_solution(16758529522129774541)
XLA Ops:
  0.6 54.4 %window_block.1 = (f32[384,192]{1,0:T(8,128)S(1)}, f32[2,12,6,192]{3,2,1,0:T(8,128)S(1)}, f32[8,48,128]{2,1,0:T(8,128)S(1)}, f32[4,16,128]{2,1,0:T(8,128)S(1)}) custom-call(f32[6,12,4,192]{3,2,1,0:T(4,128)} %bitcast.11, f32[6,12,4,192]{3,2,1,0:T(4,128)} %bitcast.12, f32[1,192]{1,0:T(1,128)} %bitcast.14, f32[1,192]{1,0:T(1,128)} %bitcast.15, ...), custom_call_target="tpu_custom_call" | custom-call | tf_op jit(solution)/shard_map/window_block/pallas_call | solution.py:544
  55.0 1.0 %unpack.1 = (f32[6,12,4,192]{3,2,1,0:T(4,128)}, f32[12,24]{1,0:T(8,128)}, f32[6,23,2,144]{3,2,1,0:T(2,128)}, f32[2,192]{1,0:T(2,128)}) custom-call(f32[384,192]{1,0:T(8,128)S(1)} %get-tuple-element.12.grad_ref, f32[2,12,6,192]{3,2,1,0:T(8,128)S(1)} %get-tuple-element.13.piece, f32[8,48,128]{2,1,0:T(8,128)S(1)} %get-tuple-element.14.gathered, ...), custom_call_target="tpu_custom_call" | custom-call | tf_op jit(solution)/shard_map/unpack/pallas_call | solution.py:600

commit v4 on v3

--- a/solution.py
+++ b/solution.py
@@ -30,6 +30,7 @@
 POS = 12
 TABW = 896
 NEG = -1e30
+FAR_FIRST = {4: (2, 1, 3), 8: (4, 3, 5, 2, 6, 1, 7)}
 PAIRS_OF_HEADS = 3
 LANES = 2 * HEAD
 F32 = jnp.float32
@@ -109,7 +110,10 @@
             turned[pl.ds(row, 24, stride=GROUP), :] = spread[c * 24 : c * 24 + 24, n * 128 : n * 128 + 128]
         for n in (6, 7, 14, 15):
             turned[pl.ds(n, 24, stride=GROUP), :] = jnp.zeros((24, 128), F32)
-        strip[c] = turned[...].T[:BLOCK, :] + strip_mask(c)
+        band = turned[...].T[:BLOCK, :] + strip_mask(c)
+        for x in range(WLON):
+            move = (WLON - 1 - x) * GROUP
+            strip[c, x] = (band if move == 0 else pltpu.roll(band, STRIP - move, 1))[:, :ROWS]
 
 
 def parity_lanes(width):
@@ -150,11 +154,66 @@
         halo_out, halo_in, win, back_out, unit, cot, inv, hid,
         qh, ql, kh, kl, vh, vl, gh_, gl_,
         strip, turned, qst, gst, scores, dattn, ah, al, dh, dl, lanes,
-        wsend, xsend, nsend, bsend, wcore, xcore, ncore, wsum, xsum, wrecv, xrecv,
+        wsend, xsend, nsend, bsend, wcore, xcore, ncore, wsum, xsum, wrecv, xrecv, nsum, nrecv,
         brecv, ypart, yrecv, zsend, zrecv, ysend,
-        send_p, recv_p, send_c, recv_c, send_h, recv_h, send_x, recv_x, send_b, recv_b,
+        send_p, recv_p, send_c, recv_c, send_h, recv_h, send_x, recv_x, send_n, recv_n, send_b, recv_b,
         send_y, recv_y, send_g, recv_g, send_z, recv_z, send_l, recv_l,
     ) = refs
+    if comm:
+        lat, lon = lax.axis_index("lat"), lax.axis_index("lon")
+    else:
+        lat, lon = jnp.int32(0), jnp.int32(0)
+    count = NZ * NY
+    z, y = lon // NY, lax.rem(lon, NY)
+    k, core = lat // 2, lax.rem(lat, 2)
+    right, left = {"lon": lax.rem(lon + 1, count)}, {"lon": lax.rem(lon + count - 1, count)}
+    partner = {"lat": k * 2 + 1 - core}
+
+    def at_k(i):
+        return {"lat": lax.rem(k + i, NK) * 2 + core}
+
+    def at_z(i):
+        return {"lon": lax.rem(z + i, NZ) * NY + y}
+
+    def at_y(i):
+        return {"lon": z * NY + lax.rem(y + i, NY)}
+
+    def remote(src, dst, send, recv, device):
+        return pltpu.make_async_remote_copy(
+            src_ref=src, dst_ref=dst, send_sem=send, recv_sem=recv, device_id=device, device_id_type=MESH
+        )
+
+    def start_all(copies):
+        for copy in copies if comm else ():
+            copy.start()
+
+    def wait_all(copies):
+        for copy in copies if comm else ():
+            copy.wait()
+
+    def exchange(n, mine, where, src, dst, send, recv):
+        for i in FAR_FIRST[n] if comm else ():
+            other = lax.rem(mine + i, n)
+            remote(src(other), dst.at[mine], send.at[i], recv.at[mine], where(i)).start()
+
+    def finish(n, mine, where, src, dst, send, recv):
+        for i in FAR_FIRST[n][::-1] if comm else ():
+            other = lax.rem(mine + i, n)
+            copy = remote(src(other), dst.at[other], send.at[i], recv.at[other], where(i))
+            copy.wait_recv()
+            copy.wait_send()
+
+    def total(ref, n):
+        return functools.reduce(lambda a, b: a + b, [ref[s] for s in range(n)])
+
+    if comm:
+        barrier = pltpu.get_barrier_semaphore()
+        everyone = [left, right]
+        everyone += [at_y(i) for i in FAR_FIRST[NY]] + [at_z(i) for i in FAR_FIRST[NZ]]
+        everyone += [at_k(i) for i in FAR_FIRST[NK]] + [partner]
+        for device in everyone:
+            pl.semaphore_signal(barrier, inc=1, device_id=device, device_id_type=MESH)
+
     loads = [
         pltpu.make_async_copy(src, dst, load_sem.at[i])
         for i, (src, dst) in enumerate(
@@ -166,76 +225,6 @@
     ]
     for load in loads:
         load.start()
-    if comm:
-        lat, lon = lax.axis_index("lat"), lax.axis_index("lon")
-    else:
-        lat, lon = jnp.int32(0), jnp.int32(0)
-    count = NZ * NY
-    z, y = lon // NY, lax.rem(lon, NY)
-    k, core = lat // 2, lax.rem(lat, 2)
-    right, left = {"lon": lax.rem(lon + 1, count)}, {"lon": lax.rem(lon + count - 1, count)}
-    partner = {"lat": k * 2 + 1 - core}
-
-    def at_k(i):
-        return {"lat": lax.rem(k + i, NK) * 2 + core}
-
-    def at_z(i):
-        return {"lon": lax.rem(z + i, NZ) * NY + y}
-
-    def at_y(i):
-        return {"lon": z * NY + lax.rem(y + i, NY)}
-
-    def remote(src, dst, send, recv, device):
-        return pltpu.make_async_remote_copy(
-            src_ref=src, dst_ref=dst, send_sem=send, recv_sem=recv, device_id=device, device_id_type=MESH
-        )
-
-    def start_all(copies):
-        for copy in copies if comm else ():
-            copy.start()
-
-    def wait_all(copies):
-        for copy in copies if comm else ():
-            copy.wait()
-
-    def exchange(n, mine, where, src, dst, send, recv):
-        def start(i, carry):
-            other = lax.rem(mine + i, n)
-            remote(src(other), dst.at[mine], send.at[i], recv.at[mine], where(i)).start()
-            return carry
-
-        if comm:
-            lax.fori_loop(1, n, start, 0)
-
-    def finish(n, mine, where, src, dst, send, recv):
-        def done(i, carry):
-            other = lax.rem(mine + i, n)
-            copy = remote(src(other), dst.at[other], send.at[i], recv.at[other], where(i))
-            copy.wait_send()
-            copy.wait_recv()
-            return carry
-
-        if comm:
-            lax.fori_loop(1, n, done, 0)
-
-    def total(ref, n):
-        return functools.reduce(lambda a, b: a + b, [ref[s] for s in range(n)])
-
-    if comm:
-        barrier = pltpu.get_barrier_semaphore()
-
-        def greet(where):
-            def step(i, carry):
-                pl.semaphore_signal(barrier, inc=1, device_id=where(i), device_id_type=MESH)
-                return carry
-
-            return step
-
-        lax.fori_loop(1, NY, greet(at_y), 0)
-        lax.fori_loop(1, NZ, greet(at_z), 0)
-        lax.fori_loop(1, NK, greet(at_k), 0)
-        for device in (left, right, partner):
-            pl.semaphore_signal(barrier, inc=1, device_id=device, device_id_type=MESH)
 
     def tiles(slabs, first):
         for x in range(HALF):
@@ -338,25 +327,36 @@
             part = nt(rows, pair_cols(vh[own, :], vl[own, :], p), None)
             dattn[w, :, p * 32 : p * 32 + 32, :] = part.reshape(WLON, 32, ROWS)
 
+    nothing = jnp.zeros((BLOCK, 128), F32)
     for w in range(PW):
-        band = strip[w]
-        dband = jnp.zeros((BLOCK, STRIP), F32)
+        turns = [None] * 8
         for x in range(WLON):
-            move = (WLON - 1 - x) * GROUP
-            bias = band if move == 0 else pltpu.roll(band, STRIP - move, 1)
-            s = scores[w, x] + bias[:, :ROWS]
+            s = scores[w, x] + strip[w, x]
             e = jnp.exp(s - jnp.max(s, axis=1, keepdims=True))
             a = e * (1.0 / jnp.sum(e, axis=1, keepdims=True))
             da = dattn[w, x]
             ds = a * (da - jnp.sum(a * da, axis=1, keepdims=True))
             ah[w, x], al[w, x] = split(a, 2)
             dh[w, x], dl[w, x] = split(ds, 2)
-            wide = jnp.concatenate([ds, jnp.zeros((BLOCK, STRIP - ROWS), F32)], axis=1)
-            dband = dband + (wide if move == 0 else pltpu.roll(wide, move, 1))
+            turn, tile = (WLON - 1 - x) % 8, (WLON - 1 - x) // 8
+            two = jnp.concatenate([ds, jnp.zeros((BLOCK, 256 - ROWS), F32)], axis=1)
+            wide = jnp.concatenate([nothing, two] if tile else [two, nothing], axis=1)
+            turns[turn] = wide if turns[turn] is None else turns[turn] + wide
+        dband = turns[0]
+        for turn in range(1, 8):
+            dband = dband + pltpu.roll(turns[turn], turn * GROUP, 1)
         turned[:, :BLOCK] = dband.T
         for n in range(POS):
             row = (n // WLAT) * 8 + n % WLAT
             lanes[pl.ds(w * 24, 24), n * 128 : n * 128 + 128] = turned[pl.ds(row, 24, stride=GROUP), :]
+
+    perm = perm_ref[...]
+    sums = sum(nn(part, perm, None) for part in split(lanes[...], 2))
+    for t in range(7):
+        bsend[t] = sums[:, t * 128 : (t + 1) * 128]
+    bsend[7] = jnp.zeros((48, 128), F32)
+    step_b = (NZ, z, at_z, lambda o: bsend.at[o], brecv, send_b, recv_b)
+    exchange(*step_b)
 
     def pair_of(ref, w, p):
         return ref[w, :, p * 32 : p * 32 + 32, :].reshape(PSTACK, ROWS)
@@ -405,14 +405,6 @@
         remote(nsend, ncore, send_c.at[2], recv_c.at[2], partner),
     ]
     start_all(swap[:1])
-
-    perm = perm_ref[...]
-    sums = sum(nn(part, perm, None) for part in split(lanes[...], 2))
-    for t in range(7):
-        bsend[t] = sums[:, t * 128 : (t + 1) * 128]
-    bsend[7] = jnp.zeros((48, 128), F32)
-    step_b = (NZ, z, at_z, lambda o: bsend.at[o], brecv, send_b, recv_b)
-    exchange(*step_b)
 
     dq = applied(dh, dl, kh, kl) * scale
     step_h = (NK, k, at_k, lambda o: wsum.at[o], wrecv, send_h, recv_h)
@@ -441,11 +433,10 @@
         axis=0,
     )
     start_all(swap[2:])
-    wait_all(swap[1:])
+    wait_all(swap[1:2])
     if comm:
         for o in range(NK):
-            xsum[o, 0:36, :] = xsend[core, o] + xcore[o]
-            xsum[o, 36:40, :] = nsend[...] + ncore[...]
+            xsum[o] = xsend[core, o] + xcore[o]
         exchange(*step_x)
         xrecv[k] = xsum[k]
 
@@ -468,6 +459,12 @@
         last[0, 0:4, :] = nsend[...]
         return
 
+    wait_all(swap[2:])
+    step_n = (NK, k, at_k, lambda o: nsum, nrecv, send_n, recv_n)
+    nsum[...] = nsend[...] + ncore[...]
+    exchange(*step_n)
+    nrecv[k] = nsum[...]
+
     step_y = (NY, y, at_y, lambda o: ypart, yrecv, send_y, recv_y)
     step_g = (NZ, z, at_z, lambda o: gathered.at[z], gathered, send_g, recv_g)
     step_z = (NZ, z, at_z, lambda o: zsend.at[o], zrecv, send_z, recv_z)
@@ -483,7 +480,8 @@
     block_vo = total(wrecv, NK)
     finish(*step_x)
     block_qk = total(xrecv, NK)
-    norm = block_qk[36:39]
+    finish(*step_n)
+    norm = total(nrecv, NK)[0:3]
     lane = lax.broadcasted_iota(jnp.int32, (12, 128), 1)
     for t in range(NZ):
         block = block_qk if t < 4 else block_vo
@@ -517,7 +515,7 @@
     hbm = pl.BlockSpec(memory_space=pltpu.HBM)
     dma = pltpu.SemaphoreType.DMA
     sems = []
-    for n in (6, 3, NK, NK, NZ, NY, NZ, NZ, NY):
+    for n in (6, 3, NK, NK, NK, NZ, NY, NZ, NZ, NY):
         sems += [dma((n,)), dma((n,))]
 
     def buf(*shape):
@@ -552,11 +550,11 @@
             buf(2, PIECES, WLAT, D),
             full, full, buf(PW * ROWS, 1), full,
             token, token, token, token, token, token, token, token,
-            buf(PW, BLOCK, STRIP), buf(STRIP, 128), stack, stack, buf(*square), buf(*square),
+            buf(*square), buf(STRIP, 128), stack, stack, buf(*square), buf(*square),
             half(*square), half(*square), half(*square), half(*square), buf(48, POS * 128),
             buf(2, NK, 36, 128), buf(2, NK, 36, 128), buf(4, 128), buf(NZ, 48, 128),
             buf(NK, 36, 128), buf(NK, 36, 128), buf(4, 128),
-            buf(NK, 36, 128), buf(NK, 40, 128), buf(NK, 36, 128), buf(NK, 40, 128),
+            buf(NK, 36, 128), buf(NK, 36, 128), buf(NK, 36, 128), buf(NK, 36, 128), buf(4, 128), buf(NK, 4, 128),
             buf(NZ, 48, 128), buf(48, 128), buf(NY, 48, 128),
             buf(NZ, 16, 128), buf(NZ, 16, 128), buf(16, 128),
         ] + sems,

time: 56.9 us -> 55.4 us (0.974)
  the two profiles are of different devices: /device:TPU:6 before, /device:TPU:16 now
where the time goes in v4:
time: 55.4 us; the launch traced here: 55.2 us
  Pallas kernels  54.6 us (99%)
  between operations  0.64 us (1%)
    pallas_call x1, Pallas kernels, main_call(): pl.pallas_call(functools.partial(main_kernel, comm), out_shape=outs, in_s...  53.6 us

profile of v4, /device:TPU:16, one launch (start us, length us, event | category | flops | bytes accessed | tf_op | source)
XLA Modules:
  0.0 55.2 jit_solution(13203539282342215591)
XLA Ops:
  0.6 53.6 %window_block.1 = (f32[384,192]{1,0:T(8,128)S(1)}, f32[2,12,6,192]{3,2,1,0:T(8,128)S(1)}, f32[8,48,128]{2,1,0:T(8,128)S(1)}, f32[4,16,128]{2,1,0:T(8,128)S(1)}) custom-call(f32[6,12,4,192]{3,2,1,0:T(4,128)} %bitcast.11, f32[6,12,4,192]{3,2,1,0:T(4,128)} %bitcast.12, f32[1,192]{1,0:T(1,128)} %bitcast.14, f32[1,192]{1,0:T(1,128)} %bitcast.15, ...), custom_call_target="tpu_custom_call" | custom-call | tf_op jit(solution)/shard_map/window_block/pallas_call | solution.py:542
  54.2 1.0 %unpack.1 = (f32[6,12,4,192]{3,2,1,0:T(4,128)}, f32[12,24]{1,0:T(8,128)}, f32[6,23,2,144]{3,2,1,0:T(2,128)}, f32[2,192]{1,0:T(2,128)}) custom-call(f32[384,192]{1,0:T(8,128)S(1)} %get-tuple-element.12.grad_ref, f32[2,12,6,192]{3,2,1,0:T(8,128)S(1)} %get-tuple-element.13.piece, f32[8,48,128]{2,1,0:T(8,128)S(1)} %get-tuple-element.14.gathered, ...), custom_call_target="tpu_custom_call" | custom-call | tf_op jit(solution)/shard_map/unpack/pallas_call | solution.py:598

commit v5 on v4

--- a/solution.py
+++ b/solution.py
@@ -30,7 +30,6 @@
 POS = 12
 TABW = 896
 NEG = -1e30
-FAR_FIRST = {4: (2, 1, 3), 8: (4, 3, 5, 2, 6, 1, 7)}
 PAIRS_OF_HEADS = 3
 LANES = 2 * HEAD
 F32 = jnp.float32
@@ -40,6 +39,12 @@
 NK = 8
 NZ = 8
 NY = 4
+FAR_FIRST = {4: (2, 1, 3), 8: (4, 3, 5, 2, 6, 1, 7)}
+NLON = NZ * NY
+AROUND = sorted(
+    ((dz, dy) for dz in range(NZ) for dy in range(NY) if dz or dy),
+    key=lambda t: -(min(t[0], NZ - t[0]) + 2 * min(t[1], NY - t[1])),
+)
 VLIM = 32 * 1024 * 1024
 
 
@@ -155,9 +160,9 @@
         qh, ql, kh, kl, vh, vl, gh_, gl_,
         strip, turned, qst, gst, scores, dattn, ah, al, dh, dl, lanes,
         wsend, xsend, nsend, bsend, wcore, xcore, ncore, wsum, xsum, wrecv, xrecv, nsum, nrecv,
-        brecv, ypart, yrecv, zsend, zrecv, ysend,
+        brecv, zsend, zrecv,
         send_p, recv_p, send_c, recv_c, send_h, recv_h, send_x, recv_x, send_n, recv_n, send_b, recv_b,
-        send_y, recv_y, send_g, recv_g, send_z, recv_z, send_l, recv_l,
+        send_g, recv_g, send_l, recv_l,
     ) = refs
     if comm:
         lat, lon = lax.axis_index("lat"), lax.axis_index("lon")
@@ -172,11 +177,8 @@
     def at_k(i):
         return {"lat": lax.rem(k + i, NK) * 2 + core}
 
-    def at_z(i):
-        return {"lon": lax.rem(z + i, NZ) * NY + y}
-
-    def at_y(i):
-        return {"lon": z * NY + lax.rem(y + i, NY)}
+    def lon_of(dz, dy):
+        return lax.rem(z + dz, NZ) * NY + lax.rem(y + dy, NY)
 
     def remote(src, dst, send, recv, device):
         return pltpu.make_async_remote_copy(
@@ -191,15 +193,16 @@
         for copy in copies if comm else ():
             copy.wait()
 
-    def exchange(n, mine, where, src, dst, send, recv):
-        for i in FAR_FIRST[n] if comm else ():
-            other = lax.rem(mine + i, n)
-            remote(src(other), dst.at[mine], send.at[i], recv.at[mine], where(i)).start()
-
-    def finish(n, mine, where, src, dst, send, recv):
-        for i in FAR_FIRST[n][::-1] if comm else ():
-            other = lax.rem(mine + i, n)
-            copy = remote(src(other), dst.at[other], send.at[i], recv.at[other], where(i))
+    lon_peers = [(lon_of(dz, dy), {"lon": lon_of(dz, dy)}) for dz, dy in AROUND]
+    k_peers = [(lax.rem(k + i, NK), at_k(i)) for i in FAR_FIRST[NK]]
+
+    def exchange(peers, mine, src, dst, send, recv):
+        for i, (other, device) in enumerate(peers if comm else ()):
+            remote(src(other), dst.at[mine], send.at[i], recv.at[mine], device).start()
+
+    def finish(peers, mine, src, dst, send, recv):
+        for i, (other, device) in list(enumerate(peers if comm else ()))[::-1]:
+            copy = remote(src(other), dst.at[other], send.at[i], recv.at[other], device)
             copy.wait_recv()
             copy.wait_send()
 
@@ -209,8 +212,8 @@
     if comm:
         barrier = pltpu.get_barrier_semaphore()
         everyone = [left, right]
-        everyone += [at_y(i) for i in FAR_FIRST[NY]] + [at_z(i) for i in FAR_FIRST[NZ]]
-        everyone += [at_k(i) for i in FAR_FIRST[NK]] + [partner]
+        everyone += [{"lon": lax.rem(lon + i, count)} for i in range(2, count - 1)]
+        everyone += [device for _, device in k_peers] + [partner]
         for device in everyone:
             pl.semaphore_signal(barrier, inc=1, device_id=device, device_id_type=MESH)
 
@@ -241,7 +244,7 @@
             for t in range(3):
                 halo_out[d, t * PIECES + g] = parts[t]
     if comm:
-        pl.semaphore_wait(barrier, 3 + NY - 1 + NZ - 1 + NK - 1)
+        pl.semaphore_wait(barrier, len(everyone))
     cuts = (pl.ds(0, 2 * PIECES), pl.ds(2 * PIECES, PIECES))
     halo = [
         [
@@ -353,9 +356,10 @@
     perm = perm_ref[...]
     sums = sum(nn(part, perm, None) for part in split(lanes[...], 2))
     for t in range(7):
-        bsend[t] = sums[:, t * 128 : (t + 1) * 128]
-    bsend[7] = jnp.zeros((48, 128), F32)
-    step_b = (NZ, z, at_z, lambda o: bsend.at[o], brecv, send_b, recv_b)
+        for q in range(NY):
+            bsend[t * NY + q] = sums[q * 12 : (q + 1) * 12, t * 128 : (t + 1) * 128]
+    bsend[pl.ds(28, 4)] = jnp.zeros((4, 12, 128), F32)
+    step_b = (lon_peers, lon, lambda o: bsend.at[o], brecv, send_b, recv_b)
     exchange(*step_b)
 
     def pair_of(ref, w, p):
@@ -407,8 +411,8 @@
     start_all(swap[:1])
 
     dq = applied(dh, dl, kh, kl) * scale
-    step_h = (NK, k, at_k, lambda o: wsum.at[o], wrecv, send_h, recv_h)
-    step_x = (NK, k, at_k, lambda o: xsum.at[o], xrecv, send_x, recv_x)
+    step_h = (k_peers, k, lambda o: wsum.at[o], wrecv, send_h, recv_h)
+    step_x = (k_peers, k, lambda o: xsum.at[o], xrecv, send_x, recv_x)
     wait_all(swap[:1])
     if comm:
         for o in range(NK):
@@ -424,14 +428,9 @@
     standard = unit[...]
     ggain = jnp.sum(gh * standard, axis=0, keepdims=True)
     gshift = jnp.sum(gh, axis=0, keepdims=True)
-    nsend[...] = jnp.concatenate(
-        [
-            ggain[:, :128], gshift[:, :128],
-            jnp.concatenate([ggain[:, 128:], gshift[:, 128:]], axis=1),
-            jnp.zeros((1, 128), F32),
-        ],
-        axis=0,
-    )
+    lead = jnp.zeros((4, 32), F32)
+    fours = [t[:, u : u + 96] for t in (ggain, gshift) for u in (0, 96)]
+    nsend[...] = jnp.concatenate([lead, jnp.concatenate(fours, axis=0)], axis=1)
     start_all(swap[2:])
     wait_all(swap[1:2])
     if comm:
@@ -456,33 +455,32 @@
         gathered[...] = bsend[...]
         spare[0] = wsend[...]
         spare[1] = xsend[...]
-        last[0, 0:4, :] = nsend[...]
+        last[0:4, :] = nsend[...]
         return
 
     wait_all(swap[2:])
-    step_n = (NK, k, at_k, lambda o: nsum, nrecv, send_n, recv_n)
+    step_n = (k_peers, k, lambda o: nsum, nrecv, send_n, recv_n)
     nsum[...] = nsend[...] + ncore[...]
     exchange(*step_n)
     nrecv[k] = nsum[...]
 
-    step_y = (NY, y, at_y, lambda o: ypart, yrecv, send_y, recv_y)
-    step_g = (NZ, z, at_z, lambda o: gathered.at[z], gathered, send_g, recv_g)
-    step_z = (NZ, z, at_z, lambda o: zsend.at[o], zrecv, send_z, recv_z)
-    step_l = (NY, y, at_y, lambda o: ysend, last, send_l, recv_l)
-
-    brecv[z] = bsend[z]
+    step_g = (lon_peers, lon, lambda o: gathered.at[lon], gathered, send_g, recv_g)
+    step_l = (lon_peers, lon, lambda o: zsend.at[o], zrecv, send_l, recv_l)
+
+    brecv[lon] = bsend[lon]
     finish(*step_b)
-    ypart[...] = total(brecv, NZ)
-    exchange(*step_y)
-    yrecv[y] = ypart[...]
+    gathered[lon] = total(brecv, NLON)
+    exchange(*step_g)
 
     finish(*step_h)
     block_vo = total(wrecv, NK)
+    finish(*step_n)
+    norm = jnp.concatenate([total(nrecv, NK), jnp.zeros((4, 128), F32)], axis=0)
     finish(*step_x)
     block_qk = total(xrecv, NK)
-    finish(*step_n)
-    norm = total(nrecv, NK)[0:3]
     lane = lax.broadcasted_iota(jnp.int32, (12, 128), 1)
+    lane8 = lax.broadcasted_iota(jnp.int32, (8, 128), 1)
+    row8 = lax.broadcasted_iota(jnp.int32, (8, 128), 0)
     for t in range(NZ):
         block = block_qk if t < 4 else block_vo
         e = (t // 2) % 2
@@ -490,24 +488,18 @@
         if t % 2:
             tail = pltpu.roll(block[24:36], 96 if e else 32, 1)
             main = jnp.where(lane < 32, pltpu.roll(main, 32, 1), tail)
-        zsend[t, 0:12, :] = main
-        zsend[t, 12:15, :] = norm
-        zsend[t, 15:16, :] = jnp.zeros((1, 128), F32)
-    exchange(*step_z)
-    zrecv[z] = zsend[z]
-
-    finish(*step_y)
-    gathered[z] = total(yrecv, NY)
-    exchange(*step_g)
-
-    finish(*step_z)
-    ysend[...] = total(zrecv, NZ)
+        top, low = main[0:8], main[4:12]
+        for q in range(NY):
+            above = top if q == 0 else pltpu.roll(top, 128 - 24 * q, 1)
+            below = pltpu.roll(low, (160 - 24 * q) % 128, 1)
+            zsend[t * NY + q] = jnp.where(lane8 < 24, above, jnp.where(row8 < 4, norm, below))
     exchange(*step_l)
-    last[y] = ysend[...]
+    zrecv[lon] = zsend[lon]
 
     wait_all(backs)
     finish(*step_g)
     finish(*step_l)
+    last[...] = total(zrecv, NLON)
 
 
 def main_call(comm, operands):
@@ -515,7 +507,7 @@
     hbm = pl.BlockSpec(memory_space=pltpu.HBM)
     dma = pltpu.SemaphoreType.DMA
     sems = []
-    for n in (6, 3, NK, NK, NK, NZ, NY, NZ, NZ, NY):
+    for n in (6, 3, NK, NK, NK, NLON, NLON, NLON):
         sems += [dma((n,)), dma((n,))]
 
     def buf(*shape):
@@ -531,8 +523,8 @@
     outs = (
         jax.ShapeDtypeStruct((PW * ROWS, D), F32),
         jax.ShapeDtypeStruct((PW, PIECES, WLAT, D), F32),
-        jax.ShapeDtypeStruct((NZ, 48, 128), F32),
-        jax.ShapeDtypeStruct((NY, 16, 128), F32),
+        jax.ShapeDtypeStruct((NLON, 12, 128), F32),
+        jax.ShapeDtypeStruct((8, 128), F32),
     )
     params = dict(vmem_limit_bytes=VLIM)
     if comm:
@@ -552,11 +544,10 @@
             token, token, token, token, token, token, token, token,
             buf(*square), buf(STRIP, 128), stack, stack, buf(*square), buf(*square),
             half(*square), half(*square), half(*square), half(*square), buf(48, POS * 128),
-            buf(2, NK, 36, 128), buf(2, NK, 36, 128), buf(4, 128), buf(NZ, 48, 128),
+            buf(2, NK, 36, 128), buf(2, NK, 36, 128), buf(4, 128), buf(NLON, 12, 128),
             buf(NK, 36, 128), buf(NK, 36, 128), buf(4, 128),
             buf(NK, 36, 128), buf(NK, 36, 128), buf(NK, 36, 128), buf(NK, 36, 128), buf(4, 128), buf(NK, 4, 128),
-            buf(NZ, 48, 128), buf(48, 128), buf(NY, 48, 128),
-            buf(NZ, 16, 128), buf(NZ, 16, 128), buf(16, 128),
+            buf(NLON, 12, 128), buf(NLON, 8, 128), buf(NLON, 8, 128),
         ] + sems,
         compiler_params=pltpu.CompilerParams(**params),
         name="window_block",
@@ -564,7 +555,6 @@
 
 
 def unpack_kernel(grad_ref, piece, gathered, last, feat_ref, weight_ref, bias_ref, norm_ref):
-    y = lax.rem(lax.axis_index("lon"), NY)
     for x in range(HALF):
         for c, slabs in ((0, (3, 0)), (1, (1, 2))):
             for i, slab in enumerate(slabs):
@@ -575,22 +565,19 @@
                 feat_ref[:, x, slab, :] = west
                 feat_ref[:, HALF + x, slab, :] = east
     for h in range(HEADS):
-        main = gathered[h]
-        rem = gathered[6]
-        rem = rem if h == 0 else pltpu.roll(rem, 128 - 16 * h, 1)
-        for c in range(PW):
-            bias_ref[h, :, c, 0:128] = main[c * 24 : c * 24 + LONREL]
-            bias_ref[h, :, c, 128:144] = rem[c * 24 : c * 24 + LONREL, :16]
-    both = functools.reduce(lambda a, b: a + b, [last[s] for s in range(NY)]) * (1.0 / 384.0)
-    rows = both[0:12]
-    mine = rows[:, 0:24]
-    for t in range(1, NY):
-        mine = jnp.where(y == t, pltpu.roll(rows, 128 - 24 * t, 1)[:, 0:24], mine)
-    weight_ref[...] = mine
-    norm_ref[0:1, 0:128] = both[12:13]
-    norm_ref[1:2, 0:128] = both[13:14]
-    norm_ref[0:1, 128:192] = both[14:15, 0:64]
-    norm_ref[1:2, 128:192] = both[14:15, 64:128]
+        for q in range(NY):
+            rows = 12 if q % 2 == 0 else LONREL - 12
+            at = pl.ds(12 * (q % 2), rows)
+            rem = gathered[24 + q]
+            rem = rem if h == 0 else pltpu.roll(rem, 128 - 16 * h, 1)
+            bias_ref[h, at, q // 2, 0:128] = gathered[h * NY + q][:rows]
+            bias_ref[h, at, q // 2, 128:144] = rem[:rows, :16]
+    both = last[...] * (1.0 / 384.0)
+    weight_ref[0:8, :] = both[:, 0:24]
+    weight_ref[8:12, :] = both[4:8, 32:56]
+    for e in range(2):
+        norm_ref[e : e + 1, 0:96] = both[2 * e : 2 * e + 1, 32:128]
+        norm_ref[e : e + 1, 96:192] = both[2 * e + 1 : 2 * e + 2, 32:128]
 
 
 def unpack(operands):

time: 55.4 us -> 56.8 us (1.025)
  the two profiles are of different devices: /device:TPU:16 before, /device:TPU:1 now
where the time goes in v5:
time: 56.8 us; the launch traced here: 56.7 us
  Pallas kernels  56 us (99%)
  between operations  0.64 us (1%)
    pallas_call x1, Pallas kernels, main_call(): pl.pallas_call(functools.partial(main_kernel, comm), out_shape=outs, in_s...  55 us

profile of v5, /device:TPU:1, one launch (start us, length us, event | category | flops | bytes accessed | tf_op | source)
XLA Modules:
  0.0 56.7 jit_solution(841890903598460031)
XLA Ops:
  0.6 55.0 %window_block.1 = (f32[384,192]{1,0:T(8,128)S(1)}, f32[2,12,6,192]{3,2,1,0:T(8,128)S(1)}, f32[32,12,128]{2,1,0:T(8,128)S(1)}, f32[8,128]{1,0:T(8,128)S(1)}) custom-call(f32[6,12,4,192]{3,2,1,0:T(4,128)} %bitcast.11, f32[6,12,4,192]{3,2,1,0:T(4,128)} %bitcast.12, f32[1,192]{1,0:T(1,128)} %bitcast.14, f32[1,192]{1,0:T(1,128)} %bitcast.15, f32[192,576]{1,0:T(8,128)} %qkv_hbm.1, ...), custom_call_target="tpu_custom_call" | custom-call | tf_op jit(solution)/shard_map/window_block/pallas_call | solution.py:534
  55.6 1.0 %unpack.1 = (f32[6,12,4,192]{3,2,1,0:T(4,128)}, f32[12,24]{1,0:T(8,128)}, f32[6,23,2,144]{3,2,1,0:T(2,128)}, f32[2,192]{1,0:T(2,128)}) custom-call(f32[384,192]{1,0:T(8,128)S(1)} %get-tuple-element.12.grad_ref, f32[2,12,6,192]{3,2,1,0:T(8,128)S(1)} %get-tuple-element.13.piece, f32[32,12,128]{2,1,0:T(8,128)S(1)} %get-tuple-element.14.gathered, ...), custom_call_target="tpu_custom_call" | custom-call | tf_op jit(solution)/shard_map/unpack/pallas_call | solution.py:585

commit v6 on v5

--- a/solution.py
+++ b/solution.py
@@ -162,7 +162,7 @@
         wsend, xsend, nsend, bsend, wcore, xcore, ncore, wsum, xsum, wrecv, xrecv, nsum, nrecv,
         brecv, zsend, zrecv,
         send_p, recv_p, send_c, recv_c, send_h, recv_h, send_x, recv_x, send_n, recv_n, send_b, recv_b,
-        send_g, recv_g, send_l, recv_l,
+        send_g, recv_g, send_s, recv_s, send_l, recv_l,
     ) = refs
     if comm:
         lat, lon = lax.axis_index("lat"), lax.axis_index("lon")
@@ -439,13 +439,25 @@
         exchange(*step_x)
         xrecv[k] = xsum[k]
 
+    mine_z = pl.ds(z * NY, NY)
+    y_peers = [(lon_of(0, i), {"lon": lon_of(0, i)}) for i in FAR_FIRST[NY]]
+    step_g = (y_peers, lon, lambda o: gathered.at[lon], gathered, send_g, recv_g)
+    if comm:
+        brecv[lon] = bsend[lon]
+        finish(*step_b)
+        gathered[lon] = total(brecv, NLON)
+        exchange(*step_g)
+
     gu = gh * gain
     mean_gu = jnp.sum(gu, axis=1, keepdims=True) * (1.0 / D)
     mean_uu = jnp.sum(gu * standard, axis=1, keepdims=True) * (1.0 / D)
     grad_ref[...] = cot[...] + inv[...] * (gu - mean_gu - standard * mean_uu)
     for d, base in ((0, 0), (1, 3 * HROWS)):
+        cells = [grad_ref[pl.ds(base + g * 8, WLAT), :] for g in range(PIECES)]
         for g in range(PIECES):
-            back_out[d, g] = grad_ref[pl.ds(base + g * 8, WLAT), :]
+            back_out[d, g] = cells[g][:, :128]
+        for g in range(HALF):
+            back_out[d, PIECES + g] = jnp.concatenate([cells[g][:, 128:], cells[HALF + g][:, 128:]], axis=1)
     backs = [
         remote(back_out.at[d], piece.at[d], send_p.at[4 + d], recv_p.at[4 + d], (left, right)[d])
         for d in range(2)
@@ -464,13 +476,15 @@
     exchange(*step_n)
     nrecv[k] = nsum[...]
 
-    step_g = (lon_peers, lon, lambda o: gathered.at[lon], gathered, send_g, recv_g)
     step_l = (lon_peers, lon, lambda o: zsend.at[o], zrecv, send_l, recv_l)
 
-    brecv[lon] = bsend[lon]
-    finish(*step_b)
-    gathered[lon] = total(brecv, NLON)
-    exchange(*step_g)
+    finish(*step_g)
+    spread_z = [
+        (remote(gathered.at[mine_z], gathered.at[mine_z], send_s.at[i], recv_s.at[z], {"lon": lon_of(dz, 0)}), dz)
+        for i, dz in enumerate(FAR_FIRST[NZ])
+    ]
+    for copy, _ in spread_z:
+        copy.start()
 
     finish(*step_h)
     block_vo = total(wrecv, NK)
@@ -497,7 +511,11 @@
     zrecv[lon] = zsend[lon]
 
     wait_all(backs)
-    finish(*step_g)
+    for i, (copy, dz) in list(enumerate(spread_z))[::-1]:
+        other = lax.rem(z + dz, NZ)
+        theirs = pl.ds(other * NY, NY)
+        remote(gathered.at[theirs], gathered.at[theirs], send_s.at[i], recv_s.at[other], {"lon": lon_of(dz, 0)}).wait_recv()
+        copy.wait_send()
     finish(*step_l)
     last[...] = total(zrecv, NLON)
 
@@ -507,7 +525,7 @@
     hbm = pl.BlockSpec(memory_space=pltpu.HBM)
     dma = pltpu.SemaphoreType.DMA
     sems = []
-    for n in (6, 3, NK, NK, NK, NLON, NLON, NLON):
+    for n in (6, 3, NK, NK, NK, NLON, NLON, NZ, NLON):
         sems += [dma((n,)), dma((n,))]
 
     def buf(*shape):
@@ -522,7 +540,7 @@
     square = (PW, WLON, BLOCK, ROWS)
     outs = (
         jax.ShapeDtypeStruct((PW * ROWS, D), F32),
-        jax.ShapeDtypeStruct((PW, PIECES, WLAT, D), F32),
+        jax.ShapeDtypeStruct((PW, PIECES + HALF, WLAT, 128), F32),
         jax.ShapeDtypeStruct((NLON, 12, 128), F32),
         jax.ShapeDtypeStruct((8, 128), F32),
     )
@@ -539,7 +557,7 @@
         scratch_shapes=[pltpu.VMEM(t.shape, t.dtype) for t in operands] + [
             dma((8,)),
             buf(2, 3 * PIECES, WLAT, 128), buf(2, 3 * PIECES, WLAT, 128), buf(3, PW * ROWS, 128),
-            buf(2, PIECES, WLAT, D),
+            buf(2, PIECES + HALF, WLAT, 128),
             full, full, buf(PW * ROWS, 1), full,
             token, token, token, token, token, token, token, token,
             buf(*square), buf(STRIP, 128), stack, stack, buf(*square), buf(*square),
@@ -560,7 +578,10 @@
             for i, slab in enumerate(slabs):
                 row = x * GROUP + i * 8
                 own = grad_ref[pl.ds((1 + c) * HROWS + row, 8), :]
-                own, far = own[:WLAT], piece[c, x * 2 + i]
+                g = x * 2 + i
+                side = piece[c, PIECES + g % HALF]
+                side = side[:, :64] if g < HALF else side[:, 64:]
+                own, far = own[:WLAT], jnp.concatenate([piece[c, g], side], axis=1)
                 west, east = (own, far) if c == 0 else (far, own)
                 feat_ref[:, x, slab, :] = west
                 feat_ref[:, HALF + x, slab, :] = east

time: 56.8 us -> 55.2 us (0.972)
  the two profiles are of different devices: /device:TPU:1 before, /device:TPU:6 now
where the time goes in v6:
time: 55.2 us; the launch traced here: 54.4 us
  Pallas kernels  53.8 us (97%)
  between operations  0.64 us (1%)
    pallas_call x1, Pallas kernels, main_call(): pl.pallas_call(functools.partial(main_kernel, comm), out_shape=outs, in_s...  52.7 us

profile of v6, /device:TPU:6, one launch (start us, length us, event | category | flops | bytes accessed | tf_op | source)
XLA Modules:
  0.0 54.4 jit_solution(13929031388518317957)
XLA Ops:
  0.6 52.7 %window_block.1 = (f32[384,192]{1,0:T(8,128)S(1)}, f32[2,18,6,128]{3,2,1,0:T(8,128)S(1)}, f32[32,12,128]{2,1,0:T(8,128)S(1)}, f32[8,128]{1,0:T(8,128)S(1)}) custom-call(f32[6,12,4,192]{3,2,1,0:T(4,128)} %bitcast.11, f32[6,12,4,192]{3,2,1,0:T(4,128)} %bitcast.12, f32[1,192]{1,0:T(1,128)} %bitcast.14, f32[1,192]{1,0:T(1,128)} %bitcast.15, f32[192,576]{1,0:T(8,128)} %qkv_hbm.1, ...), custom_call_target="tpu_custom_call" | custom-call | tf_op jit(solution)/shard_map/window_block/pallas_call | solution.py:552
  53.4 1.1 %unpack.1 = (f32[6,12,4,192]{3,2,1,0:T(4,128)}, f32[12,24]{1,0:T(8,128)}, f32[6,23,2,144]{3,2,1,0:T(2,128)}, f32[2,192]{1,0:T(2,128)}) custom-call(f32[384,192]{1,0:T(8,128)S(1)} %get-tuple-element.12.grad_ref, f32[2,18,6,128]{3,2,1,0:T(8,128)S(1)} %get-tuple-element.13.piece, f32[32,12,128]{2,1,0:T(8,128)S(1)} %get-tuple-element.14.gathered, ...), custom_call_target="tpu_custom_call" | custom-call | tf_op jit(solution)/shard_map/unpack/pallas_call | solution.py:606

commit v7 on v6

--- a/solution.py
+++ b/solution.py
@@ -442,12 +442,6 @@
     mine_z = pl.ds(z * NY, NY)
     y_peers = [(lon_of(0, i), {"lon": lon_of(0, i)}) for i in FAR_FIRST[NY]]
     step_g = (y_peers, lon, lambda o: gathered.at[lon], gathered, send_g, recv_g)
-    if comm:
-        brecv[lon] = bsend[lon]
-        finish(*step_b)
-        gathered[lon] = total(brecv, NLON)
-        exchange(*step_g)
-
     gu = gh * gain
     mean_gu = jnp.sum(gu, axis=1, keepdims=True) * (1.0 / D)
     mean_uu = jnp.sum(gu * standard, axis=1, keepdims=True) * (1.0 / D)
@@ -476,27 +470,26 @@
     exchange(*step_n)
     nrecv[k] = nsum[...]
 
+    if comm:
+        brecv[lon] = bsend[lon]
+        finish(*step_b)
+        gathered[lon] = total(brecv, NLON)
+        exchange(*step_g)
+
     step_l = (lon_peers, lon, lambda o: zsend.at[o], zrecv, send_l, recv_l)
-
-    finish(*step_g)
-    spread_z = [
-        (remote(gathered.at[mine_z], gathered.at[mine_z], send_s.at[i], recv_s.at[z], {"lon": lon_of(dz, 0)}), dz)
-        for i, dz in enumerate(FAR_FIRST[NZ])
-    ]
-    for copy, _ in spread_z:
-        copy.start()
 
     finish(*step_h)
     block_vo = total(wrecv, NK)
     finish(*step_n)
     norm = jnp.concatenate([total(nrecv, NK), jnp.zeros((4, 128), F32)], axis=0)
-    finish(*step_x)
-    block_qk = total(xrecv, NK)
     lane = lax.broadcasted_iota(jnp.int32, (12, 128), 1)
     lane8 = lax.broadcasted_iota(jnp.int32, (8, 128), 1)
     row8 = lax.broadcasted_iota(jnp.int32, (8, 128), 0)
-    for t in range(NZ):
-        block = block_qk if t < 4 else block_vo
+    block = block_vo
+    for t in (4, 5, 6, 7, 0, 1, 2, 3):
+        if t == 0:
+            finish(*step_x)
+            block = total(xrecv, NK)
         e = (t // 2) % 2
         main = block[e * 12 : e * 12 + 12]
         if t % 2:
@@ -509,6 +502,14 @@
             zsend[t * NY + q] = jnp.where(lane8 < 24, above, jnp.where(row8 < 4, norm, below))
     exchange(*step_l)
     zrecv[lon] = zsend[lon]
+
+    finish(*step_g)
+    spread_z = [
+        (remote(gathered.at[mine_z], gathered.at[mine_z], send_s.at[i], recv_s.at[z], {"lon": lon_of(dz, 0)}), dz)
+        for i, dz in enumerate(FAR_FIRST[NZ])
+    ]
+    for copy, _ in spread_z:
+        copy.start()
 
     wait_all(backs)
     for i, (copy, dz) in list(enumerate(spread_z))[::-1]:

time: 55.2 us -> 56.5 us (1.024)
  the two profiles are of different devices: /device:TPU:6 before, /device:TPU:1 now
where the time goes in v7:
time: 56.5 us; the launch traced here: 56.4 us
  Pallas kernels  55.8 us (99%)
  between operations  0.64 us (1%)
    pallas_call x1, Pallas kernels, main_call(): pl.pallas_call(functools.partial(main_kernel, comm), out_shape=outs, in_s...  54.7 us

profile of v7, /device:TPU:1, one launch (start us, length us, event | category | flops | bytes accessed | tf_op | source)
XLA Modules:
  0.0 56.4 jit_solution(15291694257033507728)
XLA Ops:
  0.6 54.7 %window_block.1 = (f32[384,192]{1,0:T(8,128)S(1)}, f32[2,18,6,128]{3,2,1,0:T(8,128)S(1)}, f32[32,12,128]{2,1,0:T(8,128)S(1)}, f32[8,128]{1,0:T(8,128)S(1)}) custom-call(f32[6,12,4,192]{3,2,1,0:T(4,128)} %bitcast.11, f32[6,12,4,192]{3,2,1,0:T(4,128)} %bitcast.12, f32[1,192]{1,0:T(1,128)} %bitcast.14, f32[1,192]{1,0:T(1,128)} %bitcast.15, f32[192,576]{1,0:T(8,128)} %qkv_hbm.1, ...), custom_call_target="tpu_custom_call" | custom-call | tf_op jit(solution)/shard_map/window_block/pallas_call | solution.py:553
  55.4 1.1 %unpack.1 = (f32[6,12,4,192]{3,2,1,0:T(4,128)}, f32[12,24]{1,0:T(8,128)}, f32[6,23,2,144]{3,2,1,0:T(2,128)}, f32[2,192]{1,0:T(2,128)}) custom-call(f32[384,192]{1,0:T(8,128)S(1)} %get-tuple-element.12.grad_ref, f32[2,18,6,128]{3,2,1,0:T(8,128)S(1)} %get-tuple-element.13.piece, f32[32,12,128]{2,1,0:T(8,128)S(1)} %get-tuple-element.14.gathered, ...), custom_call_target="tpu_custom_call" | custom-call | tf_op jit(solution)/shard_map/unpack/pallas_call | solution.py:607
